TPU v7x, 512 devices: a whole 4x4x16 slice. The times are simulated.
512 devices in a mesh: term: 16 (over y, z_hi, core), sector: 32 (over x, z_lo).
Axes of the slice: x: 4, y: 4, z: 16 (z_hi: 2, z_lo: 8; z = z_hi * 8 + z_lo), core: 2. Of those that a mesh axis runs over, the one named last changes fastest.
Arguments:
- psi_blocks: float32 [128, 128, 128], P('sector'), may hold values from -6 to 6
- left_ops: float32 [16, 128, 128, 128], P('term', 'sector'), may hold values from -0.5 to 0.5
- right_ops: float32 [16, 128, 128, 128], P('term', 'sector'), may hold values from -0.5 to 0.5
- couplings: float32 [16, 16], replicated, may hold values from -1.5 to 1.5
- pattern: int32 [16, 128], P(None, 'sector'), may hold values from 0 to 1, as said below
- channel: int32 [16], replicated, may hold values from 0 to 7
- target: int32 [128, 8], P('sector'), may hold values from 0 to 127, as said below
Outputs:
- sigma_blocks: float32 [128, 128, 128], P('sector', 'term')
Inputs may be any that keep to these rules, and one draw needn't show every extreme that they name: `pattern`: only 0 and 1. `target`: of the 32 entries of the rows 4 j to 4 j + 3, at most 2 name sectors in one aligned group of 4 sectors, and exactly 2 do for some group, for every j.
All inputs are finite; a program needn't handle non-finite values.
Results may differ from a plain program's by a relative error of at most 0.0003.
Values sent between devices are 32-bit elements; how exact they have to be, the bound alone decides.
A program may use at most 64 MiB of HBM per device.

v0:
```python
import jax
import jax.numpy as jnp
from jax import lax
from jax.sharding import PartitionSpec as P

PRECISE = lax.Precision.HIGHEST


def add_channel(totals, sector, chan_id, term_value):
    begin = (jnp.int32(sector), chan_id, jnp.int32(0), jnp.int32(0))
    current = lax.dynamic_slice(totals, begin, (1, 1) + term_value.shape)
    return lax.dynamic_update_slice(totals, current + term_value[None, None], begin)


def add_term(totals, term_id, left_tile, pattern, channel, make_inner):
    for sector in range(left_tile.shape[0]):
        is_live = pattern[term_id, sector]

        def live_path(current, sector=sector):
            inner_prod = make_inner(term_id, sector)
            term_value = jnp.dot(
                left_tile[sector], inner_prod, precision=PRECISE, preferred_element_type=jnp.float32
            )
            return add_channel(current, sector, channel[term_id], term_value)

        totals = lax.cond(is_live > 0, live_path, lambda current: current, totals)
    return totals


def sum_terms(partials):
    return lax.psum_scatter(partials, "term", scatter_dimension=2, tiled=True)


def local(psi_blocks, left_ops, right_ops, couplings, pattern, channel, target):
    sec_dev = psi_blocks.shape[0]
    block_size = psi_blocks.shape[1]
    term_dev = right_ops.shape[0]
    channels = target.shape[1]
    term_pos = lax.axis_index("term")
    zero_sum = jnp.zeros((sec_dev, channels, block_size, block_size), jnp.float32)
    own_columns = lax.dynamic_slice_in_dim(couplings, term_pos * term_dev, term_dev, 1)

    def make_inner(term_id, sector):
        partial_right = jnp.einsum(
            "b,bij->ij", own_columns[term_id], right_ops[:, sector], precision=PRECISE
        )
        return jnp.dot(
            psi_blocks[sector], partial_right, precision=PRECISE, preferred_element_type=jnp.float32
        )

    shards = lax.all_gather(left_ops, "term", axis=0, tiled=True)

    def one_term(offset, current):
        left_tile = lax.dynamic_index_in_dim(shards, offset, 0, keepdims=False)
        return add_term(current, offset, left_tile, pattern, channel, make_inner)

    partials = lax.fori_loop(0, shards.shape[0], one_term, zero_sum)
    slices = sum_terms(partials)
    share_rows = slices.shape[2]
    slot_count = sec_dev * channels
    row_length = share_rows * block_size
    flat_rows = slices.reshape(slot_count, row_length)
    targets = target.reshape(slot_count)
    owners = lax.axis_size("sector")
    capacity = max(2, (slot_count + owners - 1) // owners)
    destination = targets // sec_dev
    slot_order = jnp.arange(slot_count, dtype=jnp.int32)
    earlier = (destination[None, :] == destination[:, None]) & (
        slot_order[None, :] < slot_order[:, None]
    )
    slot_rank = jnp.sum(earlier.astype(jnp.int32), axis=1)
    position = destination * capacity + slot_rank
    buffer_rows = jnp.arange(owners * capacity, dtype=jnp.int32)
    placing = (buffer_rows[:, None] == position[None, :]).astype(jnp.float32)
    outgoing = jnp.dot(placing, flat_rows, precision=PRECISE, preferred_element_type=jnp.float32)
    labels = jnp.dot(
        placing,
        (targets % sec_dev + 1).astype(jnp.float32),
        precision=PRECISE,
        preferred_element_type=jnp.float32,
    )
    incoming, in_labels = (
        lax.all_to_all(outgoing, "sector", split_axis=0, concat_axis=0, tiled=True),
        lax.all_to_all(labels, "sector", split_axis=0, concat_axis=0, tiled=True),
    )
    local_ids = (jnp.arange(sec_dev, dtype=jnp.int32) + 1).astype(jnp.float32)
    picking = (in_labels[None, :] == local_ids[:, None]).astype(jnp.float32)
    result = jnp.dot(picking, incoming, precision=PRECISE, preferred_element_type=jnp.float32)
    return result.reshape(sec_dev, share_rows, block_size)


def solution(mesh):
    placed = (
        P("sector", None, None),
        P("term", "sector", None, None),
        P("term", "sector", None, None),
        P(),
        P(None, "sector"),
        P(),
        P("sector", None),
    )
    return jax.shard_map(
        local, mesh=mesh, in_specs=placed, out_specs=P("sector", "term", None), check_vma=False
    )
```

profile of v0, /device:TPU:1, one launch (start us, length us, event | category | flops | bytes accessed | tf_op | source)
XLA Modules:
  0.0 589.5 jit_solution(5879235126421968984)
XLA Ops:
  7.5 128.2 %all-gather.2.cloned.1.call-done = f32[16,4,128,128]{3,2,1,0:T(8,128)} async-done(((f32[1,4,128,128]{3,2,1,0:T(8,128)}), f32[16,4,128,128]{3,2,1,0:T(8,128)}) %all-gather.2.cloned.1.call-update) | async-done | bytes 4194320 | tf_op jit(solution)/shard_map/all_gather | solution.py:51
  136.0 249.1 %while.16 = (s32[]{:T(128)}, f32[4,8,128,128]{2,3,1,0:T(8,128)S(1)}, s32[16,4]{0,1:T(4,128)S(1)}, f32[16,4,128,128]{3,2,1,0:T(8,128)}, s32[16]{0:T(128)S(1)}, /*...) while((s32[]{:T(128)}, ...), condition=%wide.region_10.11_spmd, body=%wide.region_1.10_spmd.sunk | while | flops 201457696 | bytes 2360149 | solution.py:57
  138.3 4.6 conditional.8
  143.5 4.4 conditional.9
  155.9 4.6 conditional.8
  161.1 4.4 conditional.9
  173.4 4.6 conditional.8
  186.5 4.6 conditional.8
  191.8 4.4 conditional.9
  204.8 4.4 conditional.9
  210.5 4.3 conditional.11
  217.1 4.6 conditional.8
  222.3 4.4 conditional.9
  227.4 4.4 conditional.10
  239.0 4.6 conditional.8
  244.2 4.4 conditional.9
  257.8 4.4 conditional.10
  269.4 4.6 conditional.8
  274.7 4.4 conditional.9
  287.0 4.6 conditional.8
  292.2 4.4 conditional.9
  304.5 4.6 conditional.8
  309.8 4.4 conditional.9
  322.7 4.4 conditional.9
  343.6 4.6 conditional.8
  356.7 4.6 conditional.8
  362.0 4.4 conditional.9
  374.3 4.6 conditional.8
  389.3 62.2 %all-to-all-start = ((f32[32,2,1]{1,2,0:T(1,128)}), f32[32,2,1]{1,2,0:T(1,128)S(1)}, u32[]{:S(2)}, u32[]{:S(2)}) async-start(f32[32,2,1]{1,2,0:T(1,128)} %copy.24), calls=%async_computation | async-start | bytes 32768 | tf_op jit(solution)/shard_map/all_to_all | solution.py:84
  451.4 104.5 %reduce-scatter.2.cloned.1.call-done = f32[4,8,8,128]{3,1,0,2:T(8,128)} async-done(((f32[4,8,128,128]{3,1,0,2:T(8,128)}), f32[4,8,8,128]{3,1,0,2:T(8,128)}) %reduce-scatter.2.cloned.1.call-update) | async-done | bytes 131088 | tf_op jit(solution)/shard_map/reduce_scatter | solution.py:31
  558.2 5.1 all-to-all-start.1
  564.6 17.1 %all-to-all-done.1 = f32[32,2,1024]{2,1,0:T(2,128)S(1)} async-done(((f32[32,2,1024]{2,1,0:T(2,128)}), f32[32,2,1024]{2,1,0:T(2,128)S(1)}, u32[]{:S(2)}, u32[]{:S(2)}) %all-to-all-start.1) | async-done | bytes 262176 | tf_op jit(solution)/shard_map/all_to_all | solution.py:83
  (275 shorter events, 201.5 us)
Async XLA Ops:
  6.5 0.8 copy-start
  6.5 129.4 %copy-start.2 = (f32[4,128,128]{2,1,0:T(8,128)S(1)}, f32[4,128,128]{2,1,0:T(8,128)}, u32[]{:S(2)}) copy-start(f32[4,128,128]{2,1,0:T(8,128)} %param.17) | copy-start | bytes 786436
  6.5 129.4 %copy-start.1 = (f32[1,4,128,128]{3,2,1,0:T(8,128)S(1)}, f32[1,4,128,128]{3,2,1,0:T(8,128)}, u32[]{:S(2)}) copy-start(f32[1,4,128,128]{3,2,1,0:T(8,128)} %param.19) | copy-start | bytes 786436
  6.5 129.4 %copy-start.3 = (s32[16,4]{0,1:T(4,128)S(1)}, s32[16,4]{0,1:T(4,128)}, u32[]{:S(2)}) copy-start(s32[16,4]{0,1:T(4,128)} %param.21) | copy-start | bytes 772
  6.5 129.5 %copy-start.5 = (s32[16]{0:T(128)S(1)}, s32[16]{0:T(128)}, u32[]{:S(2)}) copy-start(s32[16]{0:T(128)} %param.22) | copy-start | bytes 196
  6.5 129.2 %all-gather.2.cloned.1.call-start = ((), (), s32[]{:S(2)}) async-start(), calls=%async_computation.3 | async-start | bytes 4456448 | tf_op jit(solution)/shard_map/all_gather | solution.py:51
  7.3 548.7 %reduce-scatter.2.cloned.1.call-start = ((), (), s32[]{:S(2)}) async-start(), calls=%async_computation.4 | async-start | bytes 2228224 | tf_op jit(solution)/shard_map/reduce_scatter | solution.py:31
  387.2 0.7 copy-start.4
  389.3 168.9 %all-to-all-start = ((f32[32,2,1]{1,2,0:T(1,128)}), f32[32,2,1]{1,2,0:T(1,128)S(1)}, u32[]{:S(2)}, u32[]{:S(2)}) async-start(f32[32,2,1]{1,2,0:T(1,128)} %copy.24), calls=%async_computation | async-start | bytes 32768 | tf_op jit(solution)/shard_map/all_to_all | solution.py:84
  558.2 23.5 %all-to-all-start.1 = ((f32[32,2,1024]{2,1,0:T(2,128)}), f32[32,2,1024]{2,1,0:T(2,128)S(1)}, u32[]{:S(2)}, u32[]{:S(2)}) async-start(f32[32,2,1024]{2,1,0:T(2,128)} %copy.28), calls=%async_computation.2 | async-start | bytes 524288 | tf_op jit(solution)/shard_map/all_to_all | solution.py:83
Sparse Core Ops, SparseCore 0:
  10.7 125.0 all-gather.1
  387.4 168.5 reduce-scatter.1
where the time goes:
time: 593 us; the launch traced here: 590 us
  waiting for transfers between devices  251 us (42%)
  loops' own time  122 us (21%)
  local copies, waits for them, and re-layouts  85.3 us (14%)
  starting transfers between devices  67.3 us (11%)
  matrix products  49.8 us (8%)
  between operations  13.5 us (2%)
    all_gather x1, waiting for transfers between devices, local(): shards = lax.all_gather(left_ops, 'term', axis=0, tiled=True)  128 us
    reduce_scatter x1, waiting for transfers between devices, sum_terms(): return lax.psum_scatter(partials, 'term', scatter_dimension=2, tiled=True)  105 us
    another operation x64, loops' own time, add_term(): totals = lax.cond(is_live > 0, live_path, lambda current: current, totals)  80.8 us
    all_to_all x1, starting transfers between devices, local(): lax.all_to_all(labels, 'sector', split_axis=0, concat_axis=0, tiled=True)  62.2 us
    another operation x1, loops' own time, local(): partials = lax.fori_loop(0, shards.shape[0], one_term, zero_sum)  41.4 us
    dot_general x41, matrix products, make_inner(): jnp.dot(psi_blocks[sector], partial_right, precision=PRECISE, preferred_e...  37.9 us
    dynamic_slice x41, local copies, waits for them, and re-layouts, make_inner(): own_columns[term_id]  25.9 us
    dynamic_slice x41, local copies, waits for them, and re-layouts, live_path(): return add_channel(current, sector, channel[term_id], term_value)  25.8 us
  transfers between devices with their start and end apart: 4, of which 3 were waited for; matrix products, arithmetic and copies ran while one was open for 1% of the time, Pallas kernels for 0%

commit v1 on v0

v1 whole, which is shorter than its diff:
```python
import jax
import jax.numpy as jnp
from jax import lax
from jax.sharding import PartitionSpec as P

PRECISE = lax.Precision.HIGHEST


def route_to_owners(slices, target):
    sec_dev, channels, share_rows, block_size = slices.shape
    slot_count = sec_dev * channels
    row_length = share_rows * block_size
    flat_rows = slices.reshape(slot_count, row_length)
    targets = target.reshape(slot_count)
    owners = lax.axis_size("sector")
    capacity = max(2, (slot_count + owners - 1) // owners)
    destination = targets // sec_dev
    slot_order = jnp.arange(slot_count, dtype=jnp.int32)
    earlier = (destination[None, :] == destination[:, None]) & (
        slot_order[None, :] < slot_order[:, None]
    )
    slot_rank = jnp.sum(earlier.astype(jnp.int32), axis=1)
    position = destination * capacity + slot_rank
    buffer_rows = jnp.arange(owners * capacity, dtype=jnp.int32)
    placing = (buffer_rows[:, None] == position[None, :]).astype(jnp.float32)
    outgoing = jnp.dot(placing, flat_rows, precision=PRECISE, preferred_element_type=jnp.float32)
    labels = jnp.dot(
        placing,
        (targets % sec_dev + 1).astype(jnp.float32),
        precision=PRECISE,
        preferred_element_type=jnp.float32,
    )
    incoming = lax.all_to_all(outgoing, "sector", split_axis=0, concat_axis=0, tiled=True)
    in_labels = lax.all_to_all(labels, "sector", split_axis=0, concat_axis=0, tiled=True)
    local_ids = (jnp.arange(sec_dev, dtype=jnp.int32) + 1).astype(jnp.float32)
    picking = (in_labels[None, :] == local_ids[:, None]).astype(jnp.float32)
    result = jnp.dot(picking, incoming, precision=PRECISE, preferred_element_type=jnp.float32)
    return result.reshape(sec_dev, share_rows, block_size)


def local(psi_blocks, left_ops, right_ops, couplings, pattern, channel, target):
    sec_dev, block_size, _ = psi_blocks.shape
    terms = couplings.shape[0]
    channels = target.shape[1]
    share_rows = block_size // terms

    rights = right_ops[0].reshape(sec_dev, terms, share_rows, block_size)
    rights = lax.all_to_all(rights, "term", split_axis=1, concat_axis=1, tiled=True)
    comp_rows = jnp.einsum("ab,sbrk->sark", couplings, rights, precision=PRECISE)
    comp_rows = lax.all_to_all(comp_rows, "term", split_axis=1, concat_axis=1, tiled=True)
    comp = comp_rows.reshape(sec_dev, block_size, block_size)

    inner = jnp.einsum("sij,sjk->sik", psi_blocks, comp, precision=PRECISE)
    contrib = jnp.einsum("sij,sjk->sik", left_ops[0], inner, precision=PRECISE)

    contrib = contrib.reshape(sec_dev, terms, share_rows, block_size)
    contrib = lax.all_to_all(contrib, "term", split_axis=1, concat_axis=1, tiled=True)
    chan_ids = jnp.arange(channels, dtype=jnp.int32)
    select = (channel[None, :] == chan_ids[:, None]).astype(jnp.float32)
    weights = select[None, :, :] * pattern.T.astype(jnp.float32)[:, None, :]
    partial = jnp.einsum("sca,sark->scrk", weights, contrib, precision=PRECISE)
    return route_to_owners(partial, target)


def solution(mesh):
    placed = (
        P("sector", None, None),
        P("term", "sector", None, None),
        P("term", "sector", None, None),
        P(),
        P(None, "sector"),
        P(),
        P("sector", None),
    )
    return jax.shard_map(
        local, mesh=mesh, in_specs=placed, out_specs=P("sector", "term", None), check_vma=False
    )
```

time: 593 us -> 139 us (0.23)
  waiting for transfers between devices: 251 us -> 63.7 us
  loops' own time: 122 us -> 0 us
  local copies, waits for them, and re-layouts: 85.3 us -> 6.43 us
  matrix products: 49.8 us -> 2.88 us
  starting transfers between devices: 67.3 us -> 28.7 us
  blocking collectives: 0 us -> 35.5 us
  between operations: 13.5 us -> 0.13 us
    all_gather x1 -> x0, waiting for transfers between devices: 128 us -> none  [local(): shards = lax.all_gather(left_ops, 'term', axis=0, tiled=True)]
    another operation x65 -> x0, loops' own time: 122 us -> none  [the longest x64 80.8 us: add_term(): totals = lax.cond(is_live > 0, live_path, lambda current: current, totals)]
    reduce_scatter x1 -> x0, waiting for transfers between devices: 105 us -> none  [sum_terms(): return lax.psum_scatter(partials, 'term', scatter_dimension=2, tiled=True)]
    dynamic_slice x99 -> x0, local copies, waits for them, and re-layouts: 62.4 us -> none  [the longest x41 25.9 us: make_inner(): own_columns[term_id]]
    dot_general x85 -> x7, matrix products: 49.8 us -> 2.88 us  [the longest x1 0.66 us: local(): contrib = jnp.einsum('sij,sjk->sik', left_ops[0], inner, precision=PRECISE)]
    all_to_all x2 -> x4, waiting for transfers between devices: 17.1 us -> 63.7 us  [the longest x1 22.2 us: local(): lax.all_to_all(comp_rows, 'term', split_axis=1, concat_axis=1, tiled=True)]
    all_to_all x2 -> x4, starting transfers between devices: 67.2 us -> 28.7 us  [the longest x1 14.3 us: route_to_owners(): lax.all_to_all(labels, 'sector', split_axis=0, concat_axis=0, tiled=True)]
    all_to_all x0 -> x1, blocking collectives: none -> 35.5 us  [local(): lax.all_to_all(rights, 'term', split_axis=1, concat_axis=1, tiled=True)]
  transfers between devices with their start and end apart: 4 -> 4, of which waited for: 3 -> 4; matrix products, arithmetic and copies ran while one was open for 1% -> 3% of each run, Pallas kernels for 0% -> 0%
where the time goes in v1:
time: 139 us; the launch traced here: 138 us
  waiting for transfers between devices  63.7 us (46%)
  blocking collectives  35.5 us (26%)
  starting transfers between devices  28.7 us (21%)
  local copies, waits for them, and re-layouts  6.43 us (5%)
  matrix products  2.88 us (2%)
    all_to_all x1, blocking collectives, local(): lax.all_to_all(rights, 'term', split_axis=1, concat_axis=1, tiled=True)  35.5 us
    all_to_all x1, waiting for transfers between devices, local(): lax.all_to_all(comp_rows, 'term', split_axis=1, concat_axis=1, tiled=True)  22.2 us
    all_to_all x1, waiting for transfers between devices, route_to_owners(): lax.all_to_all(outgoing, 'sector', split_axis=0, concat_axis=0, tiled=True)  17.3 us
    all_to_all x1, waiting for transfers between devices, local(): lax.all_to_all(contrib, 'term', split_axis=1, concat_axis=1, tiled=True)  14.6 us
    all_to_all x1, starting transfers between devices, route_to_owners(): lax.all_to_all(labels, 'sector', split_axis=0, concat_axis=0, tiled=True)  14.3 us
    all_to_all x1, waiting for transfers between devices, route_to_owners(): lax.all_to_all(labels, 'sector', split_axis=0, concat_axis=0, tiled=True)  9.64 us
    all_to_all x1, starting transfers between devices, local(): lax.all_to_all(contrib, 'term', split_axis=1, concat_axis=1, tiled=True)  6.08 us
    all_to_all x1, starting transfers between devices, local(): lax.all_to_all(comp_rows, 'term', split_axis=1, concat_axis=1, tiled=True)  4.43 us
  transfers between devices with their start and end apart: 4, of which 4 were waited for; matrix products, arithmetic and copies ran while one was open for 3% of the time, Pallas kernels for 0%

profile of v1, /device:TPU:1, one launch (start us, length us, event | category | flops | bytes accessed | tf_op | source)
XLA Modules:
  0.0 138.2 jit_solution(17662837238620750647)
XLA Ops:
  0.0 1.0 copy.30
  1.0 0.0 copy-start.2
  1.0 35.5 %all_to_all.30 = f32[4,16,8,128]{3,2,0,1:T(8,128)S(1)} all-to-all(f32[4,16,8,128]{3,2,0,1:T(8,128)S(1)} %copy.30), channel_id=1, replica_groups=mesh['term'=16,'sector'=32] {'term'}, dimensions={1} | all-to-all | bytes 524288 | tf_op jit(solution)/shard_map/all_to_all | solution.py:48
  36.5 0.5 convolution_bitcast_fusion.1
  37.0 0.8 copy.32
  37.8 4.4 %all-to-all-start.2 = ((f32[4,16,8,128]{3,2,0,1:T(8,128)}), f32[4,16,8,128]{3,2,0,1:T(8,128)S(1)}, u32[]{:S(2)}, u32[]{:S(2)}) async-start(f32[4,16,8,128]{3,2,0,1:T(8,128)} %copy.32), calls=%async_computation.2 | async-start | bytes 524288 | tf_op jit(solution)/shard_map/all_to_all | solution.py:50
  42.2 0.1 reshape.154
  42.3 0.1 reshape.159
  42.4 0.2 convert_reduce_fusion
  42.6 0.0 copy-start.1
  42.6 22.2 %all-to-all-done.2 = f32[4,16,8,128]{3,2,0,1:T(8,128)S(1)} async-done(((f32[4,16,8,128]{3,2,0,1:T(8,128)}), f32[4,16,8,128]{3,2,0,1:T(8,128)S(1)}, u32[]{:S(2)}, u32[]{:S(2)}) %all-to-all-start.2) | async-done | bytes 262176 | tf_op jit(solution)/shard_map/all_to_all | solution.py:50
  64.8 0.6 fusion.4
  65.4 0.7 convolution_bitcast_fusion
  66.1 0.7 copy.35
  66.8 6.1 %all-to-all-start.3 = ((f32[4,16,8,128]{3,2,0,1:T(8,128)}), f32[4,16,8,128]{3,2,0,1:T(8,128)S(1)}, u32[]{:S(2)}, u32[]{:S(2)}) async-start(f32[4,16,8,128]{3,2,0,1:T(8,128)} %copy.35), calls=%async_computation.3 | async-start | bytes 524288 | tf_op jit(solution)/shard_map/all_to_all | solution.py:57
  72.9 0.2 fusion.11
  73.1 0.8 copy.29
  73.9 0.7 copy-done.5
  74.6 14.6 %all-to-all-done.3 = f32[4,16,8,128]{3,2,0,1:T(8,128)S(1)} async-done(((f32[4,16,8,128]{3,2,0,1:T(8,128)}), f32[4,16,8,128]{3,2,0,1:T(8,128)S(1)}, u32[]{:S(2)}, u32[]{:S(2)}) %all-to-all-start.3) | async-done | bytes 262176 | tf_op jit(solution)/shard_map/all_to_all | solution.py:57
  89.1 14.3 %all-to-all-start = ((f32[32,2,1]{1,2,0:T(1,128)}), f32[32,2,1]{1,2,0:T(1,128)S(1)}, u32[]{:S(2)}, u32[]{:S(2)}) async-start(f32[32,2,1]{1,2,0:T(1,128)} %copy.29), calls=%async_computation | async-start | bytes 32768 | tf_op jit(solution)/shard_map/all_to_all | solution.py:34
  103.4 0.4 convolution_bitcast_fusion.2
  103.8 0.3 fusion.9
  104.1 0.9 copy.37
  105.0 9.6 %all-to-all-done = f32[32,2,1]{1,2,0:T(1,128)S(1)} async-done(((f32[32,2,1]{1,2,0:T(1,128)}), f32[32,2,1]{1,2,0:T(1,128)S(1)}, u32[]{:S(2)}, u32[]{:S(2)}) %all-to-all-start) | async-done | bytes 288 | tf_op jit(solution)/shard_map/all_to_all | solution.py:34
  114.7 3.9 %all-to-all-start.4 = ((f32[32,2,1024]{2,1,0:T(2,128)}), f32[32,2,1024]{2,1,0:T(2,128)S(1)}, u32[]{:S(2)}, u32[]{:S(2)}) async-start(f32[32,2,1024]{2,1,0:T(2,128)} %copy.37), calls=%async_computation.4 | async-start | bytes 524288 | tf_op jit(solution)/shard_map/all_to_all | solution.py:33
  118.6 0.5 broadcast.158
  119.1 0.7 reduce.3
  119.8 0.1 eq.82
  119.9 17.3 %all-to-all-done.4 = f32[32,2,1024]{2,1,0:T(2,128)S(1)} async-done(((f32[32,2,1024]{2,1,0:T(2,128)}), f32[32,2,1024]{2,1,0:T(2,128)S(1)}, u32[]{:S(2)}, u32[]{:S(2)}) %all-to-all-start.4) | async-done | bytes 262176 | tf_op jit(solution)/shard_map/all_to_all | solution.py:33
  137.2 0.2 all_to_all.24
  137.4 0.2 fusion
  137.6 0.6 copy.39
  (16 shorter events, 0.1 us)
Async XLA Ops:
  0.0 64.8 %copy-start = (f32[4,128,128]{2,1,0:T(8,128)S(1)}, f32[4,128,128]{2,1,0:T(8,128)}, u32[]{:S(2)}) copy-start(f32[4,128,128]{2,1,0:T(8,128)} %param.7) | copy-start | bytes 786436
  1.0 35.5 %copy-start.2 = (f32[16,16]{1,0:T(8,128)S(1)}, f32[16,16]{1,0:T(8,128)}, u32[]{:S(2)}) copy-start(f32[16,16]{1,0:T(8,128)} %param.10) | copy-start | bytes 3076
  37.8 4.4 %copy-start.3 = (s32[4,8]{1,0:T(4,128)S(1)}, s32[4,8]{1,0:T(4,128)}, u32[]{:S(2)}) copy-start(s32[4,8]{1,0:T(4,128)} %param.13) | copy-start | bytes 388
  37.8 27.0 %all-to-all-start.2 = ((f32[4,16,8,128]{3,2,0,1:T(8,128)}), f32[4,16,8,128]{3,2,0,1:T(8,128)S(1)}, u32[]{:S(2)}, u32[]{:S(2)}) async-start(f32[4,16,8,128]{3,2,0,1:T(8,128)} %copy.32), calls=%async_computation.2 | async-start | bytes 524288 | tf_op jit(solution)/shard_map/all_to_all | solution.py:50
  42.6 22.8 %copy-start.1 = (f32[1,4,128,128]{3,2,1,0:T(8,128)S(1)}, f32[1,4,128,128]{3,2,1,0:T(8,128)}, u32[]{:S(2)}) copy-start(f32[1,4,128,128]{3,2,1,0:T(8,128)} %param.8) | copy-start | bytes 786436
  66.8 22.3 %all-to-all-start.3 = ((f32[4,16,8,128]{3,2,0,1:T(8,128)}), f32[4,16,8,128]{3,2,0,1:T(8,128)S(1)}, u32[]{:S(2)}, u32[]{:S(2)}) async-start(f32[4,16,8,128]{3,2,0,1:T(8,128)} %copy.35), calls=%async_computation.3 | async-start | bytes 524288 | tf_op jit(solution)/shard_map/all_to_all | solution.py:57
  73.1 0.8 copy-start.4
  73.9 0.7 copy-start.5
  89.1 25.6 %all-to-all-start = ((f32[32,2,1]{1,2,0:T(1,128)}), f32[32,2,1]{1,2,0:T(1,128)S(1)}, u32[]{:S(2)}, u32[]{:S(2)}) async-start(f32[32,2,1]{1,2,0:T(1,128)} %copy.29), calls=%async_computation | async-start | bytes 32768 | tf_op jit(solution)/shard_map/all_to_all | solution.py:34
  114.7 22.5 %all-to-all-start.4 = ((f32[32,2,1024]{2,1,0:T(2,128)}), f32[32,2,1024]{2,1,0:T(2,128)S(1)}, u32[]{:S(2)}, u32[]{:S(2)}) async-start(f32[32,2,1024]{2,1,0:T(2,128)} %copy.37), calls=%async_computation.4 | async-start | bytes 524288 | tf_op jit(solution)/shard_map/all_to_all | solution.py:33

commit v2 on v1

--- a/solution.py
+++ b/solution.py
@@ -1,9 +1,61 @@
+import functools
+
 import jax
 import jax.numpy as jnp
 from jax import lax
+from jax.experimental import pallas as pl
+from jax.experimental.pallas import tpu as pltpu
 from jax.sharding import PartitionSpec as P
 
+MESH = pl.DeviceIdType.MESH
+
 PRECISE = lax.Precision.HIGHEST
+
+
+def exchange_kernel(axis, n, split, x_ref, o_ref, send_sem, recv_sem, local_sem):
+    me = lax.axis_index(axis)
+    barrier = pltpu.get_barrier_semaphore()
+    for k in range(1, n):
+        pl.semaphore_signal(barrier, inc=1, device_id={axis: lax.rem(me + k, n)}, device_id_type=MESH)
+    pl.semaphore_wait(barrier, n - 1)
+
+    def part(ref, idx):
+        return ref.at[idx] if split == 0 else ref.at[:, idx]
+
+    local = pltpu.make_async_copy(part(x_ref, me), part(o_ref, me), local_sem)
+    local.start()
+    copies = []
+    for k in range(1, n):
+        peer = lax.rem(me + k, n)
+        copy = pltpu.make_async_remote_copy(
+            src_ref=part(x_ref, peer),
+            dst_ref=part(o_ref, me),
+            send_sem=send_sem.at[k],
+            recv_sem=recv_sem.at[k],
+            device_id={axis: peer},
+            device_id_type=MESH,
+        )
+        copy.start()
+        copies.append(copy)
+    local.wait()
+    for copy in copies:
+        copy.wait()
+
+
+def exchange(x, axis, split, collective_id):
+    n = x.shape[split]
+    return pl.pallas_call(
+        functools.partial(exchange_kernel, axis, n, split),
+        out_shape=jax.ShapeDtypeStruct(x.shape, x.dtype),
+        in_specs=[pl.BlockSpec(memory_space=pltpu.VMEM)],
+        out_specs=pl.BlockSpec(memory_space=pltpu.VMEM),
+        scratch_shapes=[
+            pltpu.SemaphoreType.DMA((n,)),
+            pltpu.SemaphoreType.DMA((n,)),
+            pltpu.SemaphoreType.DMA(()),
+        ],
+        compiler_params=pltpu.CompilerParams(collective_id=collective_id, has_side_effects=True),
+    )(x)
 
 
 def route_to_owners(slices, target):
@@ -30,8 +82,13 @@
         precision=PRECISE,
         preferred_element_type=jnp.float32,
     )
-    incoming = lax.all_to_all(outgoing, "sector", split_axis=0, concat_axis=0, tiled=True)
-    in_labels = lax.all_to_all(labels, "sector", split_axis=0, concat_axis=0, tiled=True)
+    slot_rows = outgoing.reshape(owners, capacity * share_rows, block_size)
+    label_row = jnp.zeros((owners, 8, block_size), jnp.float32)
+    label_row = label_row.at[:, 0, :capacity].set(labels.reshape(owners, capacity))
+    packed = jnp.concatenate([slot_rows, label_row], axis=1)
+    packed = exchange(packed, "sector", 0, 3)
+    incoming = packed[:, : capacity * share_rows].reshape(owners * capacity, row_length)
+    in_labels = packed[:, capacity * share_rows, :capacity].reshape(owners * capacity)
     local_ids = (jnp.arange(sec_dev, dtype=jnp.int32) + 1).astype(jnp.float32)
     picking = (in_labels[None, :] == local_ids[:, None]).astype(jnp.float32)
     result = jnp.dot(picking, incoming, precision=PRECISE, preferred_element_type=jnp.float32)
@@ -45,16 +102,16 @@
     share_rows = block_size // terms
 
     rights = right_ops[0].reshape(sec_dev, terms, share_rows, block_size)
-    rights = lax.all_to_all(rights, "term", split_axis=1, concat_axis=1, tiled=True)
+    rights = exchange(rights, "term", 1, 0)
     comp_rows = jnp.einsum("ab,sbrk->sark", couplings, rights, precision=PRECISE)
-    comp_rows = lax.all_to_all(comp_rows, "term", split_axis=1, concat_axis=1, tiled=True)
+    comp_rows = exchange(comp_rows, "term", 1, 1)
     comp = comp_rows.reshape(sec_dev, block_size, block_size)
 
     inner = jnp.einsum("sij,sjk->sik", psi_blocks, comp, precision=PRECISE)
     contrib = jnp.einsum("sij,sjk->sik", left_ops[0], inner, precision=PRECISE)
 
     contrib = contrib.reshape(sec_dev, terms, share_rows, block_size)
-    contrib = lax.all_to_all(contrib, "term", split_axis=1, concat_axis=1, tiled=True)
+    contrib = exchange(contrib, "term", 1, 2)
     chan_ids = jnp.arange(channels, dtype=jnp.int32)
     select = (channel[None, :] == chan_ids[:, None]).astype(jnp.float32)
     weights = select[None, :, :] * pattern.T.astype(jnp.float32)[:, None, :]

time: 139 us -> 116 us (0.83)
  Pallas kernels: 0 us -> 103 us
  waiting for transfers between devices: 63.7 us -> 0 us
  blocking collectives: 35.5 us -> 0 us
  starting transfers between devices: 28.7 us -> 0 us
  matrix products: 2.88 us -> 6.1 us
  local copies, waits for them, and re-layouts: 6.43 us -> 4.99 us
    pallas_call x0 -> x4, Pallas kernels: none -> 103 us  [exchange(): pl.pallas_call(functools.partial(exchange_kernel, axis, n, split), out_sh...]
    all_to_all x4 -> x0, waiting for transfers between devices: 63.7 us -> none  [the longest x1 22.2 us: local(): lax.all_to_all(comp_rows, 'term', split_axis=1, concat_axis=1, tiled=True)]
    all_to_all x1 -> x0, blocking collectives: 35.5 us -> none  [local(): lax.all_to_all(rights, 'term', split_axis=1, concat_axis=1, tiled=True)]
    all_to_all x4 -> x0, starting transfers between devices: 28.7 us -> none  [the longest x1 14.3 us: route_to_owners(): lax.all_to_all(labels, 'sector', split_axis=0, concat_axis=0, tiled=True)]
    slice x0 -> x3, local copies, waits for them, and re-layouts: none -> 1.89 us  [the longest x1 0.95 us: route_to_owners(): packed[:, capacity * share_rows, :capacity].reshape(owners * capacity)]
  transfers between devices with their start and end apart: 4 -> 0, of which waited for: 4 -> 0; matrix products, arithmetic and copies ran while one was open for 3% -> 0% of each run, Pallas kernels for 0% -> 0%
where the time goes in v2:
time: 116 us
  Pallas kernels  103 us (89%)
  matrix products  6.1 us (5%)
  local copies, waits for them, and re-layouts  4.99 us (4%)
  other arithmetic  1.85 us (2%)
    pallas_call x4, Pallas kernels, exchange(): pl.pallas_call(functools.partial(exchange_kernel, axis, n, split), out_sh...  103 us

profile of v2, /device:TPU:1, one launch (start us, length us, event | category | flops | bytes accessed | tf_op | source)
XLA Modules:
  0.0 115.9 jit_solution(4629859570784672835)
XLA Ops:
  0.0 0.0 copy-start
  0.0 0.7 fusion.22
  0.7 0.1 reshape.186
  0.8 0.6 copy-done.3
  1.4 0.1 reshape.177
  1.5 0.2 convert_reduce_fusion
  1.7 0.1 broadcast_compare_fusion
  1.8 0.1 fusion.10
  2.0 0.1 copy.23
  2.1 0.0 copy-start.2
  2.1 25.4 %shard_map.73 = f32[4,16,8,128]{3,2,1,0:T(8,128)} custom-call(f32[4,16,8,128]{3,2,1,0:T(8,128)} %bitcast.48), custom_call_target="tpu_custom_call" | custom-call | tf_op jit(solution)/shard_map/pallas_call | solution.py:47
  27.4 0.0 copy-done.2
  27.4 1.3 %fusion.7 = f32[4,8,128,16]{2,3,1,0:T(8,128)S(1)} fusion(f32[4,16,8,128]{3,2,1,0:T(8,128)} %shard_map.73, f32[16,16]{1,0:T(8,128)S(1)} %copy-done.2), kind=kOutput, calls=%fused_computation.12 | convolution fusion | flops 12582912 | bytes 525312 | tf_op jit(solution)/shard_map/ab,sbrk->sark/dot_general | solution.py:106
  28.8 0.8 copy.43
  29.5 19.8 %shard_map.74 = f32[4,16,8,128]{3,2,1,0:T(8,128)} custom-call(f32[4,16,8,128]{3,2,1,0:T(8,128)} %bitcast.47), custom_call_target="tpu_custom_call" | custom-call | tf_op jit(solution)/shard_map/pallas_call | solution.py:47
  49.3 0.0 copy-done
  49.3 0.0 copy-start.1
  49.3 1.6 %fusion.4 = f32[4,128,128]{2,1,0:T(8,128)S(1)} fusion(f32[4,128,128]{2,1,0:T(8,128)S(1)} %copy-done, f32[4,16,8,128]{3,2,1,0:T(8,128)} %shard_map.74), kind=kOutput, calls=%fused_computation.8 | convolution fusion | flops 100663296 | bytes 786432 | tf_op jit(solution)/shard_map/sij,sjk->sik/dot_general | solution.py:110
  50.9 1.3 %convolution_bitcast_fusion.x_ref = f32[4,16,8,128]{3,2,1,0:T(8,128)} fusion(f32[4,128,128]{2,1,0:T(8,128)S(1)} %fusion.4, f32[1,4,128,128]{3,2,1,0:T(8,128)S(1)} %copy-done.1), kind=kOutput, calls=%fused_computation | convolution fusion | flops 100663296 | bytes 786432 | tf_op jit(solution)/shard_map/sij,sjk->sik/dot_general | solution.py:111
  52.3 19.4 %shard_map.75 = f32[4,16,8,128]{3,2,1,0:T(8,128)} custom-call(f32[4,16,8,128]{3,2,1,0:T(8,128)} %convolution_bitcast_fusion.x_ref), custom_call_target="tpu_custom_call" | custom-call | tf_op jit(solution)/shard_map/pallas_call | solution.py:47
  71.7 0.0 copy-start.5
  71.7 0.6 copy-done.5
  72.3 1.2 %convolution_bitcast_fusion.1 = f32[32,1024]{1,0:T(8,128)S(1)} fusion(f32[4,16,8,128]{3,2,1,0:T(8,128)} %shard_map.75, f32[4,16]{1,0:T(4,128)S(1)} %convert_bitcast_fusion, f32[8,16]{1,0:T(8,128)S(1)} %fusion.19), kind=kOutput, calls=%fused_computation.1 | convolution fusion | flops 6291968 | bytes 393984 | tf_op jit(solution)/shard_map/sca,sark->scrk/dot_general | solution.py:118
  73.6 0.3 fusion.9
  73.9 0.8 select_maximum_fusion.x_ref
  74.7 38.3 %shard_map.76 = f32[32,24,128]{2,1,0:T(8,128)} custom-call(f32[32,24,128]{2,1,0:T(8,128)} %select_maximum_fusion.x_ref), custom_call_target="tpu_custom_call" | custom-call | tf_op jit(solution)/shard_map/pallas_call | solution.py:47
  113.0 0.9 slice_reduce_fusion
  114.0 0.1 eq.92
  114.1 0.0 slice-start
  114.1 0.9 slice-done
  115.1 0.2 fusion
  115.3 0.6 copy.25
  (12 shorter events, 0.1 us)
Async XLA Ops:
  0.0 49.3 %copy-start = (f32[4,128,128]{2,1,0:T(8,128)S(1)}, f32[4,128,128]{2,1,0:T(8,128)}, u32[]{:S(2)}) copy-start(f32[4,128,128]{2,1,0:T(8,128)} %param.9) | copy-start | bytes 786436
  0.7 0.7 copy-start.3
  2.1 25.4 %copy-start.2 = (f32[16,16]{1,0:T(8,128)S(1)}, f32[16,16]{1,0:T(8,128)}, u32[]{:S(2)}) copy-start(f32[16,16]{1,0:T(8,128)} %param.12) | copy-start | bytes 3076
  49.3 1.6 %copy-start.1 = (f32[1,4,128,128]{3,2,1,0:T(8,128)S(1)}, f32[1,4,128,128]{3,2,1,0:T(8,128)}, u32[]{:S(2)}) copy-start(f32[1,4,128,128]{3,2,1,0:T(8,128)} %param.10) | copy-start | bytes 786436
  52.3 19.4 %copy-start.4 = (s32[16,4]{0,1:T(4,128)S(1)}, s32[16,4]{0,1:T(4,128)}, u32[]{:S(2)}) copy-start(s32[16,4]{0,1:T(4,128)} %param.13) | copy-start | bytes 772
  71.7 0.7 copy-start.5
  114.1 1.0 slice-start

commit v3 on v2

--- a/solution.py
+++ b/solution.py
@@ -83,7 +83,7 @@
         preferred_element_type=jnp.float32,
     )
     slot_rows = outgoing.reshape(owners, capacity * share_rows, block_size)
-    label_row = jnp.zeros((owners, 8, block_size), jnp.float32)
+    label_row = jnp.zeros((owners, 1, block_size), jnp.float32)
     label_row = label_row.at[:, 0, :capacity].set(labels.reshape(owners, capacity))
     packed = jnp.concatenate([slot_rows, label_row], axis=1)
     packed = exchange(packed, "sector", 0, 3)

time: 116 us -> 111 us (0.957)
  Pallas kernels: 103 us -> 97.8 us
    pallas_call x4, Pallas kernels: 103 us -> 97.8 us  [exchange(): pl.pallas_call(functools.partial(exchange_kernel, axis, n, split), out_sh...]
where the time goes in v3:
time: 111 us
  Pallas kernels  97.8 us (88%)
  matrix products  6.1 us (5%)
  local copies, waits for them, and re-layouts  4.99 us (4%)
  other arithmetic  1.85 us (2%)
    pallas_call x4, Pallas kernels, exchange(): pl.pallas_call(functools.partial(exchange_kernel, axis, n, split), out_sh...  97.8 us

profile of v3, /device:TPU:1, one launch (start us, length us, event | category | flops | bytes accessed | tf_op | source)
XLA Modules:
  0.0 110.9 jit_solution(6422356713343724046)
XLA Ops:
  0.0 0.0 copy-start
  0.0 0.7 fusion.22
  0.7 0.1 reshape.186
  0.8 0.6 copy-done.3
  1.4 0.1 reshape.177
  1.5 0.2 convert_reduce_fusion
  1.7 0.1 broadcast_compare_fusion
  1.8 0.1 fusion.10
  2.0 0.1 copy.23
  2.1 0.0 copy-start.2
  2.1 25.4 %shard_map.73 = f32[4,16,8,128]{3,2,1,0:T(8,128)} custom-call(f32[4,16,8,128]{3,2,1,0:T(8,128)} %bitcast.48), custom_call_target="tpu_custom_call" | custom-call | tf_op jit(solution)/shard_map/pallas_call | solution.py:47
  27.4 0.0 copy-done.2
  27.4 1.3 %fusion.7 = f32[4,8,128,16]{2,3,1,0:T(8,128)S(1)} fusion(f32[4,16,8,128]{3,2,1,0:T(8,128)} %shard_map.73, f32[16,16]{1,0:T(8,128)S(1)} %copy-done.2), kind=kOutput, calls=%fused_computation.12 | convolution fusion | flops 12582912 | bytes 525312 | tf_op jit(solution)/shard_map/ab,sbrk->sark/dot_general | solution.py:106
  28.8 0.8 copy.43
  29.5 19.8 %shard_map.74 = f32[4,16,8,128]{3,2,1,0:T(8,128)} custom-call(f32[4,16,8,128]{3,2,1,0:T(8,128)} %bitcast.47), custom_call_target="tpu_custom_call" | custom-call | tf_op jit(solution)/shard_map/pallas_call | solution.py:47
  49.3 0.0 copy-done
  49.3 0.0 copy-start.1
  49.3 1.6 %fusion.4 = f32[4,128,128]{2,1,0:T(8,128)S(1)} fusion(f32[4,128,128]{2,1,0:T(8,128)S(1)} %copy-done, f32[4,16,8,128]{3,2,1,0:T(8,128)} %shard_map.74), kind=kOutput, calls=%fused_computation.8 | convolution fusion | flops 100663296 | bytes 786432 | tf_op jit(solution)/shard_map/sij,sjk->sik/dot_general | solution.py:110
  50.9 1.3 %convolution_bitcast_fusion.x_ref = f32[4,16,8,128]{3,2,1,0:T(8,128)} fusion(f32[4,128,128]{2,1,0:T(8,128)S(1)} %fusion.4, f32[1,4,128,128]{3,2,1,0:T(8,128)S(1)} %copy-done.1), kind=kOutput, calls=%fused_computation | convolution fusion | flops 100663296 | bytes 786432 | tf_op jit(solution)/shard_map/sij,sjk->sik/dot_general | solution.py:111
  52.3 19.4 %shard_map.75 = f32[4,16,8,128]{3,2,1,0:T(8,128)} custom-call(f32[4,16,8,128]{3,2,1,0:T(8,128)} %convolution_bitcast_fusion.x_ref), custom_call_target="tpu_custom_call" | custom-call | tf_op jit(solution)/shard_map/pallas_call | solution.py:47
  71.7 0.0 copy-start.5
  71.7 0.6 copy-done.5
  72.3 1.2 %convolution_bitcast_fusion.1 = f32[32,1024]{1,0:T(8,128)S(1)} fusion(f32[4,16,8,128]{3,2,1,0:T(8,128)} %shard_map.75, f32[4,16]{1,0:T(4,128)S(1)} %convert_bitcast_fusion, f32[8,16]{1,0:T(8,128)S(1)} %fusion.19), kind=kOutput, calls=%fused_computation.1 | convolution fusion | flops 6291968 | bytes 393984 | tf_op jit(solution)/shard_map/sca,sark->scrk/dot_general | solution.py:118
  73.6 0.3 fusion.9
  73.9 0.8 select_maximum_fusion.x_ref
  74.7 33.3 %shard_map.76 = f32[32,17,128]{2,1,0:T(8,128)} custom-call(f32[32,17,128]{2,1,0:T(8,128)} %select_maximum_fusion.x_ref), custom_call_target="tpu_custom_call" | custom-call | tf_op jit(solution)/shard_map/pallas_call | solution.py:47
  108.0 0.9 slice_reduce_fusion
  109.0 0.1 eq.92
  109.1 0.0 slice-start
  109.1 0.9 slice-done
  110.1 0.2 fusion
  110.3 0.6 copy.25
  (12 shorter events, 0.1 us)
Async XLA Ops:
  0.0 49.3 %copy-start = (f32[4,128,128]{2,1,0:T(8,128)S(1)}, f32[4,128,128]{2,1,0:T(8,128)}, u32[]{:S(2)}) copy-start(f32[4,128,128]{2,1,0:T(8,128)} %param.9) | copy-start | bytes 786436
  0.7 0.7 copy-start.3
  2.1 25.4 %copy-start.2 = (f32[16,16]{1,0:T(8,128)S(1)}, f32[16,16]{1,0:T(8,128)}, u32[]{:S(2)}) copy-start(f32[16,16]{1,0:T(8,128)} %param.12) | copy-start | bytes 3076
  49.3 1.6 %copy-start.1 = (f32[1,4,128,128]{3,2,1,0:T(8,128)S(1)}, f32[1,4,128,128]{3,2,1,0:T(8,128)}, u32[]{:S(2)}) copy-start(f32[1,4,128,128]{3,2,1,0:T(8,128)} %param.10) | copy-start | bytes 786436
  52.3 19.4 %copy-start.4 = (s32[16,4]{0,1:T(4,128)S(1)}, s32[16,4]{0,1:T(4,128)}, u32[]{:S(2)}) copy-start(s32[16,4]{0,1:T(4,128)} %param.13) | copy-start | bytes 772
  71.7 0.7 copy-start.5
  109.1 1.0 slice-start

commit v4 on v3

--- a/solution.py
+++ b/solution.py
@@ -1,4 +1,5 @@
 import functools
+import math
 
 import jax
 import jax.numpy as jnp
@@ -58,6 +59,105 @@
     )(x)
 
 
+def rows_of(index, share_rows):
+    return pl.ds(pl.multiple_of(index * share_rows, share_rows), share_rows)
+
+
+def term_kernel(
+    n, r_ref, l_ref, psi_ref, coup_ref, wts_ref, out_ref,
+    got_right, comp_rows, comp, contrib, got_contrib, send_sem, recv_sem, local_sem,
+):
+    me = lax.axis_index("term")
+    sec_dev, _, share_rows, block_size = got_right.shape
+    channels = out_ref.shape[1]
+    barrier = pltpu.get_barrier_semaphore()
+    for k in range(1, n):
+        pl.semaphore_signal(barrier, inc=1, device_id={"term": lax.rem(me + k, n)}, device_id_type=MESH)
+    pl.semaphore_wait(barrier, n - 1)
+
+    def send(stage, s, src_of, dst):
+        local = pltpu.make_async_copy(src_of(me), dst, local_sem.at[stage, s])
+        local.start()
+        copies = [local]
+        for k in range(1, n):
+            peer = lax.rem(me + k, n)
+            copy = pltpu.make_async_remote_copy(
+                src_ref=src_of(peer),
+                dst_ref=dst,
+                send_sem=send_sem.at[stage, s, k],
+                recv_sem=recv_sem.at[stage, s, k],
+                device_id={"term": peer},
+                device_id_type=MESH,
+            )
+            copy.start()
+            copies.append(copy)
+        return copies
+
+    def arrived(copies):
+        copies[0].wait()
+        for copy in copies[1:]:
+            copy.wait_recv()
+
+    def gathered(buf, s, k):
+        return buf[s, lax.rem(me + k, n)]
+
+    first = [send(0, s, lambda p, s=s: r_ref.at[s, rows_of(p, share_rows)], got_right.at[s, me]) for s in range(sec_dev)]
+    second = []
+    for s in range(sec_dev):
+        arrived(first[s])
+        parts = [gathered(got_right, s, k) for k in range(n)]
+        for a in range(n):
+            total = coup_ref[a * n] * parts[0]
+            for k in range(1, n):
+                total = total + coup_ref[a * n + k] * parts[k]
+            comp_rows[s, a] = total
+        second.append(send(1, s, lambda p, s=s: comp_rows.at[s, p], comp.at[s, rows_of(me, share_rows)]))
+    third = []
+    for s in range(sec_dev):
+        arrived(second[s])
+        inner = jnp.dot(psi_ref[s], comp[s], precision=PRECISE, preferred_element_type=jnp.float32)
+        contrib[s] = jnp.dot(l_ref[s], inner, precision=PRECISE, preferred_element_type=jnp.float32)
+        third.append(send(2, s, lambda p, s=s: contrib.at[s, rows_of(p, share_rows)], got_contrib.at[s, me]))
+    for s in range(sec_dev):
+        arrived(third[s])
+        parts = [gathered(got_contrib, s, k) for k in range(n)]
+        for c in range(channels):
+            base = (s * channels + c) * n
+            total = wts_ref[base] * parts[0]
+            for k in range(1, n):
+                total = total + wts_ref[base + k] * parts[k]
+            out_ref[s, c] = total
+    for copies in first + second + third:
+        for copy in copies[1:]:
+            copy.wait_send()
+
+
+def term_stage(rights, lefts, psi_blocks, coup, wts, channels):
+    sec_dev, block_size, _ = psi_blocks.shape
+    n = math.isqrt(coup.shape[0])
+    share_rows = block_size // n
+    tiles = (sec_dev, n, share_rows, block_size)
+    vmem = pl.BlockSpec(memory_space=pltpu.VMEM)
+    smem = pl.BlockSpec(memory_space=pltpu.SMEM)
+    return pl.pallas_call(
+        functools.partial(term_kernel, n),
+        out_shape=jax.ShapeDtypeStruct((sec_dev, channels, share_rows, block_size), jnp.float32),
+        in_specs=[vmem, vmem, vmem, smem, smem],
+        out_specs=vmem,
+        scratch_shapes=[
+            pltpu.VMEM(tiles, jnp.float32),
+            pltpu.VMEM(tiles, jnp.float32),
+            pltpu.VMEM((sec_dev, block_size, block_size), jnp.float32),
+            pltpu.VMEM((sec_dev, block_size, block_size), jnp.float32),
+            pltpu.VMEM(tiles, jnp.float32),
+            pltpu.SemaphoreType.DMA((3, sec_dev, n)),
+            pltpu.SemaphoreType.DMA((3, sec_dev, n)),
+            pltpu.SemaphoreType.DMA((3, sec_dev)),
+        ],
+        compiler_params=pltpu.CompilerParams(collective_id=0, has_side_effects=True),
+    )(rights, lefts, psi_blocks, coup, wts)
+
+
 def route_to_owners(slices, target):
     sec_dev, channels, share_rows, block_size = slices.shape
     slot_count = sec_dev * channels
@@ -86,7 +186,7 @@
     label_row = jnp.zeros((owners, 1, block_size), jnp.float32)
     label_row = label_row.at[:, 0, :capacity].set(labels.reshape(owners, capacity))
     packed = jnp.concatenate([slot_rows, label_row], axis=1)
-    packed = exchange(packed, "sector", 0, 3)
+    packed = exchange(packed, "sector", 0, 1)
     incoming = packed[:, : capacity * share_rows].reshape(owners * capacity, row_length)
     in_labels = packed[:, capacity * share_rows, :capacity].reshape(owners * capacity)
     local_ids = (jnp.arange(sec_dev, dtype=jnp.int32) + 1).astype(jnp.float32)
@@ -96,26 +196,16 @@
 
 
 def local(psi_blocks, left_ops, right_ops, couplings, pattern, channel, target):
-    sec_dev, block_size, _ = psi_blocks.shape
     terms = couplings.shape[0]
     channels = target.shape[1]
-    share_rows = block_size // terms
-
-    rights = right_ops[0].reshape(sec_dev, terms, share_rows, block_size)
-    rights = exchange(rights, "term", 1, 0)
-    comp_rows = jnp.einsum("ab,sbrk->sark", couplings, rights, precision=PRECISE)
-    comp_rows = exchange(comp_rows, "term", 1, 1)
-    comp = comp_rows.reshape(sec_dev, block_size, block_size)
-
-    inner = jnp.einsum("sij,sjk->sik", psi_blocks, comp, precision=PRECISE)
-    contrib = jnp.einsum("sij,sjk->sik", left_ops[0], inner, precision=PRECISE)
-
-    contrib = contrib.reshape(sec_dev, terms, share_rows, block_size)
-    contrib = exchange(contrib, "term", 1, 2)
+    me = lax.axis_index("term")
+    order = lax.rem(me + jnp.arange(terms, dtype=jnp.int32), terms)
+    coup = couplings[:, order].reshape(-1)
     chan_ids = jnp.arange(channels, dtype=jnp.int32)
     select = (channel[None, :] == chan_ids[:, None]).astype(jnp.float32)
     weights = select[None, :, :] * pattern.T.astype(jnp.float32)[:, None, :]
-    partial = jnp.einsum("sca,sark->scrk", weights, contrib, precision=PRECISE)
+    wts = weights[:, :, order].reshape(-1)
+    partial = term_stage(right_ops[0], left_ops[0], psi_blocks, coup, wts, channels)
     return route_to_owners(partial, target)
 
 

time: 111 us -> 103 us (0.928); the launches traced: 111 us -> 102 us
  Pallas kernels: 97.8 us -> 90.5 us
  matrix products: 6.1 us -> 1.52 us
  local copies, waits for them, and re-layouts: 4.99 us -> 7.61 us
    pallas_call x4 -> x1, Pallas kernels: 97.8 us -> 31.2 us  [exchange(): pl.pallas_call(functools.partial(exchange_kernel, axis, n, split), out_sh...]
    pallas_call x0 -> x1, Pallas kernels: none -> 59.4 us  [term_stage(): pl.pallas_call(functools.partial(term_kernel, n), out_shape=jax.ShapeDtyp...]
    dot_general x4 -> x0, matrix products: 5.48 us -> none  [the longest x1 1.59 us: local(): inner = jnp.einsum('sij,sjk->sik', psi_blocks, comp, precision=PRECISE)]
    reshape x0 -> x2, local copies, waits for them, and re-layouts: none -> 1.33 us  [the longest x1 0.66 us: local(): wts = weights[:, :, order].reshape(-1)]
    gather x0 -> x4, local copies, waits for them, and re-layouts: none -> 1.3 us  [the longest x2 0.67 us: local(): wts = weights[:, :, order].reshape(-1)]
where the time goes in v4:
time: 103 us; the launch traced here: 102 us
  Pallas kernels  90.5 us (88%)
  local copies, waits for them, and re-layouts  7.61 us (7%)
  other arithmetic  1.94 us (2%)
  matrix products  1.52 us (1%)
    pallas_call x1, Pallas kernels, term_stage(): pl.pallas_call(functools.partial(term_kernel, n), out_shape=jax.ShapeDtyp...  59.4 us
    pallas_call x1, Pallas kernels, exchange(): pl.pallas_call(functools.partial(exchange_kernel, axis, n, split), out_sh...  31.2 us

profile of v4, /device:TPU:1, one launch (start us, length us, event | category | flops | bytes accessed | tf_op | source)
XLA Modules:
  0.0 101.7 jit_solution(18445324475214356113)
XLA Ops:
  0.0 0.7 fusion.13
  0.7 0.0 copy-start
  0.7 0.1 reshape.234
  0.8 0.6 copy-done
  1.4 0.1 reshape.211
  1.5 0.2 convert_reduce_fusion
  1.7 0.1 broadcast_compare_fusion
  1.8 0.1 fusion.6
  1.9 0.2 copy.28
  2.1 0.6 copy-done.1
  2.7 0.1 copy.24
  2.8 0.6 gather_fusion
  3.3 0.1 copy.25
  3.4 0.7 reshape.212.coup_ref
  4.1 0.0 copy-done.2
  4.1 0.1 copy.26
  4.2 0.6 copy-done.3
  4.8 0.1 fusion.10
  4.8 0.1 broadcast_multiply_fusion
  4.9 0.6 gather_fusion.1
  5.5 0.1 copy.27
  5.6 0.7 reshape.213.wts_ref
  6.3 59.4 %shard_map.73 = f32[4,8,8,128]{3,2,1,0:T(8,128)} custom-call(f32[4,128,128]{2,1,0:T(8,128)} %bitcast.29, f32[4,128,128]{2,1,0:T(8,128)} %bitcast.30, f32[4,128,128]{2,1,0:T(8,128)} %psi_ref.1, f32[256]{0:T(256)} %reshape.212.coup_ref, f32[512]{0:T(512)} %reshape.213.wts_ref), custom_call_target="tpu_custom_call" | custom-call | tf_op jit(solution)/shard_map/pallas_call | solution.py:142
  65.6 1.2 %fusion.3 = f32[64,1024]{1,0:T(8,128)S(1)} fusion(f32[4,8,8,128]{3,2,1,0:T(8,128)} %shard_map.73, s32[32]{0:T(128)S(1)} %multiply_add_fusion.1), kind=kOutput, calls=%fused_computation.7 | convolution fusion | flops 25167872 | bytes 393344 | tf_op jit(solution)/shard_map/dot_general | solution.py:178
  66.8 0.8 select_maximum_fusion.x_ref
  67.6 31.2 %shard_map.74 = f32[32,17,128]{2,1,0:T(8,128)} custom-call(f32[32,17,128]{2,1,0:T(8,128)} %select_maximum_fusion.x_ref), custom_call_target="tpu_custom_call" | custom-call | tf_op jit(solution)/shard_map/pallas_call | solution.py:48
  98.8 0.9 slice_reduce_fusion
  99.8 0.1 eq.92
  99.9 0.0 slice-start
  99.9 0.9 slice-done
  100.9 0.2 fusion
  101.1 0.6 copy.30
  (12 shorter events, 0.2 us)
Async XLA Ops:
  0.7 0.7 copy-start
  1.9 0.8 copy-start.1
  3.4 0.7 copy-start.2
  4.1 0.7 copy-start.3
  99.9 1.0 slice-start

commit v5 on v4

--- a/solution.py
+++ b/solution.py
@@ -1,5 +1,4 @@
 import functools
-import math
 
 import jax
 import jax.numpy as jnp
@@ -64,8 +63,8 @@
 
 
 def term_kernel(
-    n, r_ref, l_ref, psi_ref, coup_ref, wts_ref, out_ref,
-    got_right, comp_rows, comp, contrib, got_contrib, send_sem, recv_sem, local_sem,
+    n, r_ref, l_hbm, psi_hbm, coup_ref, pattern_ref, channel_ref, out_ref,
+    l_ref, psi_ref, got_right, comp_rows, comp, contrib, got_contrib, send_sem, recv_sem, local_sem, load_sem,
 ):
     me = lax.axis_index("term")
     sec_dev, _, share_rows, block_size = got_right.shape
@@ -101,17 +100,22 @@
     def gathered(buf, s, k):
         return buf[s, lax.rem(me + k, n)]
 
+    loads = [pltpu.make_async_copy(l_hbm, l_ref, load_sem.at[0]), pltpu.make_async_copy(psi_hbm, psi_ref, load_sem.at[1])]
+    for load in loads:
+        load.start()
     first = [send(0, s, lambda p, s=s: r_ref.at[s, rows_of(p, share_rows)], got_right.at[s, me]) for s in range(sec_dev)]
     second = []
     for s in range(sec_dev):
         arrived(first[s])
         parts = [gathered(got_right, s, k) for k in range(n)]
         for a in range(n):
-            total = coup_ref[a * n] * parts[0]
+            total = coup_ref[a, me] * parts[0]
             for k in range(1, n):
-                total = total + coup_ref[a * n + k] * parts[k]
+                total = total + coup_ref[a, lax.rem(me + k, n)] * parts[k]
             comp_rows[s, a] = total
         second.append(send(1, s, lambda p, s=s: comp_rows.at[s, p], comp.at[s, rows_of(me, share_rows)]))
+    for load in loads:
+        load.wait()
     third = []
     for s in range(sec_dev):
         arrived(second[s])
@@ -122,40 +126,45 @@
         arrived(third[s])
         parts = [gathered(got_contrib, s, k) for k in range(n)]
         for c in range(channels):
-            base = (s * channels + c) * n
-            total = wts_ref[base] * parts[0]
-            for k in range(1, n):
-                total = total + wts_ref[base + k] * parts[k]
+            total = None
+            for k in range(n):
+                term = lax.rem(me + k, n)
+                live = jnp.where(channel_ref[term] == c, pattern_ref[term, s], 0).astype(jnp.float32)
+                total = live * parts[k] if total is None else total + live * parts[k]
             out_ref[s, c] = total
     for copies in first + second + third:
         for copy in copies[1:]:
             copy.wait_send()
 
 
-def term_stage(rights, lefts, psi_blocks, coup, wts, channels):
+def term_stage(rights, lefts, psi_blocks, couplings, pattern, channel, channels):
     sec_dev, block_size, _ = psi_blocks.shape
-    n = math.isqrt(coup.shape[0])
+    n = couplings.shape[0]
     share_rows = block_size // n
     tiles = (sec_dev, n, share_rows, block_size)
-    vmem = pl.BlockSpec(memory_space=pltpu.VMEM)
+    blocks = (sec_dev, block_size, block_size)
+    hbm = pl.BlockSpec(memory_space=pl.ANY)
     smem = pl.BlockSpec(memory_space=pltpu.SMEM)
     return pl.pallas_call(
         functools.partial(term_kernel, n),
         out_shape=jax.ShapeDtypeStruct((sec_dev, channels, share_rows, block_size), jnp.float32),
-        in_specs=[vmem, vmem, vmem, smem, smem],
-        out_specs=vmem,
+        in_specs=[hbm, hbm, hbm, smem, smem, smem],
+        out_specs=pl.BlockSpec(memory_space=pltpu.VMEM),
         scratch_shapes=[
+            pltpu.VMEM(blocks, jnp.float32),
+            pltpu.VMEM(blocks, jnp.float32),
             pltpu.VMEM(tiles, jnp.float32),
             pltpu.VMEM(tiles, jnp.float32),
-            pltpu.VMEM((sec_dev, block_size, block_size), jnp.float32),
-            pltpu.VMEM((sec_dev, block_size, block_size), jnp.float32),
+            pltpu.VMEM(blocks, jnp.float32),
+            pltpu.VMEM(blocks, jnp.float32),
             pltpu.VMEM(tiles, jnp.float32),
             pltpu.SemaphoreType.DMA((3, sec_dev, n)),
             pltpu.SemaphoreType.DMA((3, sec_dev, n)),
             pltpu.SemaphoreType.DMA((3, sec_dev)),
+            pltpu.SemaphoreType.DMA((2,)),
         ],
         compiler_params=pltpu.CompilerParams(collective_id=0, has_side_effects=True),
-    )(rights, lefts, psi_blocks, coup, wts)
+    )(rights, lefts, psi_blocks, couplings, pattern, channel)
 
 
 def route_to_owners(slices, target):
@@ -196,16 +205,8 @@
 
 
 def local(psi_blocks, left_ops, right_ops, couplings, pattern, channel, target):
-    terms = couplings.shape[0]
     channels = target.shape[1]
-    me = lax.axis_index("term")
-    order = lax.rem(me + jnp.arange(terms, dtype=jnp.int32), terms)
-    coup = couplings[:, order].reshape(-1)
-    chan_ids = jnp.arange(channels, dtype=jnp.int32)
-    select = (channel[None, :] == chan_ids[:, None]).astype(jnp.float32)
-    weights = select[None, :, :] * pattern.T.astype(jnp.float32)[:, None, :]
-    wts = weights[:, :, order].reshape(-1)
-    partial = term_stage(right_ops[0], left_ops[0], psi_blocks, coup, wts, channels)
+    partial = term_stage(right_ops[0], left_ops[0], psi_blocks, couplings, pattern, channel, channels)
     return route_to_owners(partial, target)
 
 

time: 103 us -> 99.8 us (0.969)
  local copies, waits for them, and re-layouts: 7.61 us -> 4.99 us
    reshape x2 -> x0, local copies, waits for them, and re-layouts: 1.33 us -> none  [the longest x1 0.66 us: local(): wts = weights[:, :, order].reshape(-1)]
    gather x4 -> x0, local copies, waits for them, and re-layouts: 1.3 us -> none  [the longest x2 0.67 us: local(): wts = weights[:, :, order].reshape(-1)]
where the time goes in v5:
time: 99.8 us; the launch traced here: 98.9 us
  Pallas kernels  90.5 us (91%)
  local copies, waits for them, and re-layouts  4.99 us (5%)
  other arithmetic  1.78 us (2%)
  matrix products  1.52 us (2%)
    pallas_call x1, Pallas kernels, term_stage(): pl.pallas_call(functools.partial(term_kernel, n), out_shape=jax.ShapeDtyp...  59.8 us
    pallas_call x1, Pallas kernels, exchange(): pl.pallas_call(functools.partial(exchange_kernel, axis, n, split), out_sh...  30.7 us
    unnamed x5, local copies, waits for them, and re-layouts  2.03 us

profile of v5, /device:TPU:1, one launch (start us, length us, event | category | flops | bytes accessed | tf_op | source)
XLA Modules:
  0.0 98.9 jit_solution(13453619664968586625)
XLA Ops:
  0.0 0.7 fusion.12
  0.7 0.0 copy-start
  0.7 0.1 reshape.153
  0.8 0.6 copy-done
  1.4 0.1 reshape.148
  1.5 0.2 convert_reduce_fusion
  1.7 0.1 broadcast_compare_fusion
  1.8 0.1 fusion.6
  1.9 0.1 copy.16
  2.0 0.0 copy-start.1
  2.0 0.7 copy-done.1
  2.8 0.7 copy.15.pattern_ref
  3.5 59.8 %shard_map.73 = f32[4,8,8,128]{3,2,1,0:T(8,128)} custom-call(f32[4,128,128]{2,1,0:T(8,128)} %bitcast.23, f32[4,128,128]{2,1,0:T(8,128)} %bitcast.24, f32[4,128,128]{2,1,0:T(8,128)} %psi_hbm.1, f32[16,16]{1,0:T(8,128)} %coup_ref.1, s32[16,4]{1,0:T(8,128)} %copy.15.pattern_ref, s32[16]{0:T(128)} %channel_ref.1), custom_call_target="tpu_custom_call" | custom-call | tf_op jit(solution)/shard_map/pallas_call | solution.py:148
  63.3 1.2 %fusion.3 = f32[64,1024]{1,0:T(8,128)S(1)} fusion(f32[4,8,8,128]{3,2,1,0:T(8,128)} %shard_map.73, s32[32]{0:T(128)S(1)} %multiply_add_fusion.1), kind=kOutput, calls=%fused_computation.5 | convolution fusion | flops 25167872 | bytes 393344 | tf_op jit(solution)/shard_map/dot_general | solution.py:187
  64.5 0.8 select_maximum_fusion.x_ref
  65.3 30.7 %shard_map.74 = f32[32,17,128]{2,1,0:T(8,128)} custom-call(f32[32,17,128]{2,1,0:T(8,128)} %select_maximum_fusion.x_ref), custom_call_target="tpu_custom_call" | custom-call | tf_op jit(solution)/shard_map/pallas_call | solution.py:47
  95.9 0.9 slice_reduce_fusion
  96.9 0.1 eq.72
  97.0 0.0 slice-start
  97.0 0.9 slice-done
  98.0 0.2 fusion
  98.2 0.6 copy.18
  (6 shorter events, 0.1 us)
Async XLA Ops:
  0.7 0.7 copy-start
  2.0 0.8 copy-start.1
  97.0 1.0 slice-start

commit v6 on v5

v6 whole, which is shorter than its diff:
```python
import functools

import jax
import jax.numpy as jnp
from jax import lax
from jax.experimental import pallas as pl
from jax.experimental.pallas import tpu as pltpu
from jax.sharding import PartitionSpec as P

MESH = pl.DeviceIdType.MESH

PRECISE = lax.Precision.HIGHEST


def rows_of(index, share_rows):
    return pl.ds(pl.multiple_of(index * share_rows, share_rows), share_rows)


def term_kernel(
    n, owners, r_ref, l_hbm, psi_hbm, coup_ref, pattern_ref, channel_ref, source_ref, keep_ref, label_ref,
    got_slots, got_labels,
    l_ref, psi_ref, got_right, comp_rows, comp, contrib, got_contrib, partial, outgoing,
    send_sem, recv_sem, local_sem, load_sem, route_sem, label_sem,
):
    me = lax.axis_index("term")
    here = lax.axis_index("sector")
    sec_dev, _, share_rows, block_size = got_right.shape
    channels = partial.shape[0] // sec_dev
    capacity = outgoing.shape[1] // share_rows
    barrier = pltpu.get_barrier_semaphore()
    for k in range(1, n):
        pl.semaphore_signal(barrier, inc=1, device_id={"term": lax.rem(me + k, n)}, device_id_type=MESH)
    for k in range(1, owners):
        pl.semaphore_signal(barrier, inc=1, device_id={"sector": lax.rem(here + k, owners)}, device_id_type=MESH)
    pl.semaphore_wait(barrier, n - 1 + owners - 1)

    def route(src_of, dst, sems, local):
        first = pltpu.make_async_copy(src_of(here), dst, local)
        first.start()
        copies = [first]
        for k in range(1, owners):
            peer = lax.rem(here + k, owners)
            copy = pltpu.make_async_remote_copy(
                src_ref=src_of(peer),
                dst_ref=dst,
                send_sem=sems.at[0, k],
                recv_sem=sems.at[1, k],
                device_id={"sector": peer},
                device_id_type=MESH,
            )
            copy.start()
            copies.append(copy)
        return copies

    labels = route(lambda p: label_ref.at[p], got_labels.at[here], label_sem, load_sem.at[2])

    def send(stage, s, src_of, dst):
        local = pltpu.make_async_copy(src_of(me), dst, local_sem.at[stage, s])
        local.start()
        copies = [local]
        for k in range(1, n):
            peer = lax.rem(me + k, n)
            copy = pltpu.make_async_remote_copy(
                src_ref=src_of(peer),
                dst_ref=dst,
                send_sem=send_sem.at[stage, s, k],
                recv_sem=recv_sem.at[stage, s, k],
                device_id={"term": peer},
                device_id_type=MESH,
            )
            copy.start()
            copies.append(copy)
        return copies

    def arrived(copies):
        copies[0].wait()
        for copy in copies[1:]:
            copy.wait_recv()

    def gathered(buf, s, k):
        return buf[s, lax.rem(me + k, n)]

    loads = [pltpu.make_async_copy(l_hbm, l_ref, load_sem.at[0]), pltpu.make_async_copy(psi_hbm, psi_ref, load_sem.at[1])]
    for load in loads:
        load.start()
    first = [send(0, s, lambda p, s=s: r_ref.at[s, rows_of(p, share_rows)], got_right.at[s, me]) for s in range(sec_dev)]
    second = []
    for s in range(sec_dev):
        arrived(first[s])
        parts = [gathered(got_right, s, k) for k in range(n)]
        for a in range(n):
            total = coup_ref[a, me] * parts[0]
            for k in range(1, n):
                total = total + coup_ref[a, lax.rem(me + k, n)] * parts[k]
            comp_rows[s, a] = total
        second.append(send(1, s, lambda p, s=s: comp_rows.at[s, p], comp.at[s, rows_of(me, share_rows)]))
    for load in loads:
        load.wait()
    third = []
    for s in range(sec_dev):
        arrived(second[s])
        inner = jnp.dot(psi_ref[s], comp[s], precision=PRECISE, preferred_element_type=jnp.float32)
        contrib[s] = jnp.dot(l_ref[s], inner, precision=PRECISE, preferred_element_type=jnp.float32)
        third.append(send(2, s, lambda p, s=s: contrib.at[s, rows_of(p, share_rows)], got_contrib.at[s, me]))
    for s in range(sec_dev):
        arrived(third[s])
        parts = [gathered(got_contrib, s, k) for k in range(n)]
        for c in range(channels):
            total = None
            for k in range(n):
                term = lax.rem(me + k, n)
                live = jnp.where(channel_ref[term] == c, pattern_ref[term, s], 0).astype(jnp.float32)
                total = live * parts[k] if total is None else total + live * parts[k]
            partial[s * channels + c] = total
    for o in range(owners):
        for slot in range(capacity):
            at = o * capacity + slot
            outgoing[o, pl.ds(slot * share_rows, share_rows)] = keep_ref[at] * partial[source_ref[at]]
    fourth = route(lambda p: outgoing.at[p], got_slots.at[here], route_sem, load_sem.at[3])
    for copies in (labels, fourth):
        arrived(copies)
    for copies in first + second + third + [labels, fourth]:
        for copy in copies[1:]:
            copy.wait_send()


def term_stage(rights, lefts, psi_blocks, couplings, pattern, channel, source, keep, label_rows, channels):
    sec_dev, block_size, _ = psi_blocks.shape
    n = couplings.shape[0]
    owners = label_rows.shape[0]
    capacity = source.shape[0] // owners
    share_rows = block_size // n
    tiles = (sec_dev, n, share_rows, block_size)
    blocks = (sec_dev, block_size, block_size)
    routed = (owners, capacity * share_rows, block_size)
    hbm = pl.BlockSpec(memory_space=pl.ANY)
    smem = pl.BlockSpec(memory_space=pltpu.SMEM)
    vmem = pl.BlockSpec(memory_space=pltpu.VMEM)
    return pl.pallas_call(
        functools.partial(term_kernel, n, owners),
        out_shape=(
            jax.ShapeDtypeStruct(routed, jnp.float32),
            jax.ShapeDtypeStruct(label_rows.shape, jnp.float32),
        ),
        in_specs=[hbm, hbm, hbm, smem, smem, smem, smem, smem, vmem],
        out_specs=(vmem, vmem),
        scratch_shapes=[
            pltpu.VMEM(blocks, jnp.float32),
            pltpu.VMEM(blocks, jnp.float32),
            pltpu.VMEM(tiles, jnp.float32),
            pltpu.VMEM(tiles, jnp.float32),
            pltpu.VMEM(blocks, jnp.float32),
            pltpu.VMEM(blocks, jnp.float32),
            pltpu.VMEM(tiles, jnp.float32),
            pltpu.VMEM((sec_dev * channels, share_rows, block_size), jnp.float32),
            pltpu.VMEM(routed, jnp.float32),
            pltpu.SemaphoreType.DMA((3, sec_dev, n)),
            pltpu.SemaphoreType.DMA((3, sec_dev, n)),
            pltpu.SemaphoreType.DMA((3, sec_dev)),
            pltpu.SemaphoreType.DMA((4,)),
            pltpu.SemaphoreType.DMA((2, owners)),
            pltpu.SemaphoreType.DMA((2, owners)),
        ],
        compiler_params=pltpu.CompilerParams(collective_id=0, has_side_effects=True),
    )(rights, lefts, psi_blocks, couplings, pattern, channel, source, keep, label_rows)


def slot_tables(target, owners):
    sec_dev, channels = target.shape
    slot_count = sec_dev * channels
    targets = target.reshape(slot_count)
    capacity = max(2, (slot_count + owners - 1) // owners)
    destination = targets // sec_dev
    slot_order = jnp.arange(slot_count, dtype=jnp.int32)
    earlier = (destination[None, :] == destination[:, None]) & (slot_order[None, :] < slot_order[:, None])
    position = destination * capacity + jnp.sum(earlier.astype(jnp.int32), axis=1)
    buffer_rows = jnp.arange(owners * capacity, dtype=jnp.int32)
    placing = buffer_rows[:, None] == position[None, :]
    keep = jnp.any(placing, axis=1)
    source = jnp.sum(jnp.where(placing, slot_order[None, :], 0), axis=1)
    labels = jnp.sum(jnp.where(placing, (targets % sec_dev + 1)[None, :], 0), axis=1)
    label_rows = jnp.zeros((owners, 1, 128), jnp.float32)
    label_rows = label_rows.at[:, 0, :capacity].set(labels.reshape(owners, capacity).astype(jnp.float32))
    return source.astype(jnp.int32), keep.astype(jnp.float32), label_rows


def pick_arrivals(got_slots, got_labels, sec_dev, capacity):
    owners, rows, block_size = got_slots.shape
    share_rows = rows // capacity
    incoming = got_slots.reshape(owners * capacity, share_rows * block_size)
    in_labels = got_labels[:, 0, :capacity].reshape(owners * capacity)
    local_ids = (jnp.arange(sec_dev, dtype=jnp.int32) + 1).astype(jnp.float32)
    picking = (in_labels[None, :] == local_ids[:, None]).astype(jnp.float32)
    result = jnp.dot(picking, incoming, precision=PRECISE, preferred_element_type=jnp.float32)
    return result.reshape(sec_dev, share_rows, block_size)


def local(psi_blocks, left_ops, right_ops, couplings, pattern, channel, target):
    sec_dev, channels = target.shape
    owners = lax.axis_size("sector")
    source, keep, label_rows = slot_tables(target, owners)
    got_slots, got_labels = term_stage(
        right_ops[0], left_ops[0], psi_blocks, couplings, pattern, channel, source, keep, label_rows, channels
    )
    return pick_arrivals(got_slots, got_labels, sec_dev, source.shape[0] // owners)


def solution(mesh):
    placed = (
        P("sector", None, None),
        P("term", "sector", None, None),
        P("term", "sector", None, None),
        P(),
        P(None, "sector"),
        P(),
        P("sector", None),
    )
    return jax.shard_map(
        local, mesh=mesh, in_specs=placed, out_specs=P("sector", "term", None), check_vma=False
    )
```

time: 99.8 us -> 90.7 us (0.909)
  Pallas kernels: 90.5 us -> 83.4 us
  matrix products: 1.52 us -> 0.22 us
    pallas_call x2 -> x1, Pallas kernels: 90.5 us -> 83.4 us  [term_stage(): pl.pallas_call(functools.partial(term_kernel, n, owners), out_shape=(jax....]
    dot_general x3 -> x1, matrix products: 1.52 us -> 0.22 us  [pick_arrivals(): jnp.dot(picking, incoming, precision=PRECISE, preferred_element_type=jnp....]
    slice x3 -> x1, local copies, waits for them, and re-layouts: 1.89 us -> 0.76 us  [pick_arrivals(): in_labels = got_labels[:, 0, :capacity].reshape(owners * capacity)]
where the time goes in v6:
time: 90.7 us; the launch traced here: 90.4 us
  Pallas kernels  83.4 us (92%)
  local copies, waits for them, and re-layouts  5.32 us (6%)
  other arithmetic  1.47 us (2%)
    pallas_call x1, Pallas kernels, term_stage(): pl.pallas_call(functools.partial(term_kernel, n, owners), out_shape=(jax....  83.4 us
    unnamed x5, local copies, waits for them, and re-layouts  2.04 us

profile of v6, /device:TPU:1, one launch (start us, length us, event | category | flops | bytes accessed | tf_op | source)
XLA Modules:
  0.0 90.4 jit_solution(16528096593094342030)
XLA Ops:
  0.0 0.0 copy-start.1
  0.0 0.7 copy-done.1
  0.7 0.1 reshape.150
  0.8 0.2 convert_reduce_fusion
  1.0 0.1 fusion.3
  1.1 0.6 convert_element_type.26.keep_ref
  1.7 0.6 select_reduce_fusion
  2.2 0.0 copy-start
  2.2 0.7 copy-done
  2.9 0.7 copy.16.pattern_ref
  3.6 0.1 convert_element_type.28
  3.7 0.6 scatter.4.label_ref
  4.3 83.4 %shard_map.73 = (f32[32,16,128]{2,1,0:T(8,128)}, f32[32,1,128]{2,1,0:T(1,128)}) custom-call(f32[4,128,128]{2,1,0:T(8,128)} %bitcast.14, f32[4,128,128]{2,1,0:T(8,128)} %bitcast.15, f32[4,128,128]{2,1,0:T(8,128)} %psi_hbm.1, f32[16,16]{1,0:T(8,128)} %coup_ref.1, s32[16,4]{1,0:T(8,128)} %copy.16.pattern_ref, s32[16]{0:T(128)} %channel_ref.1, ...), custom_call_target="tpu_custom_call" | custom-call | tf_op jit(solution)/shard_map/pallas_call | solution.py:139
  87.7 0.8 slice_reduce_fusion
  88.4 0.1 eq.49
  88.6 1.0 %reshape.151 = f32[64,1024]{1,0:T(8,128)S(1)} reshape(f32[32,16,128]{2,1,0:T(8,128)} %get-tuple-element.20) | data formatting | bytes 524288 | tf_op jit(solution)/shard_map/reshape | solution.py:190
  89.6 0.2 fusion
  89.8 0.6 copy.18
  (4 shorter events, 0.0 us)
Async XLA Ops:
  0.0 0.7 copy-start.1
  2.2 0.7 copy-start

commit v7 on v6

--- a/solution.py
+++ b/solution.py
@@ -17,7 +17,7 @@
 
 
 def term_kernel(
-    n, owners, r_ref, l_hbm, psi_hbm, coup_ref, pattern_ref, channel_ref, source_ref, keep_ref, label_ref,
+    n, owners, r_ref, l_hbm, psi_hbm, coup_ref, pattern_ref, channel_ref, source_ref, label_ref,
     got_slots, got_labels,
     l_ref, psi_ref, got_right, comp_rows, comp, contrib, got_contrib, partial, outgoing,
     send_sem, recv_sem, local_sem, load_sem, route_sem, label_sem,
@@ -25,7 +25,7 @@
     me = lax.axis_index("term")
     here = lax.axis_index("sector")
     sec_dev, _, share_rows, block_size = got_right.shape
-    channels = partial.shape[0] // sec_dev
+    channels = (partial.shape[0] - 1) // sec_dev
     capacity = outgoing.shape[1] // share_rows
     barrier = pltpu.get_barrier_semaphore()
     for k in range(1, n):
@@ -109,13 +109,14 @@
             total = None
             for k in range(n):
                 term = lax.rem(me + k, n)
-                live = jnp.where(channel_ref[term] == c, pattern_ref[term, s], 0).astype(jnp.float32)
+                live = jnp.where(channel_ref[term] == c, pattern_ref[s, term], 0).astype(jnp.float32)
                 total = live * parts[k] if total is None else total + live * parts[k]
             partial[s * channels + c] = total
+    partial[sec_dev * channels] = jnp.zeros((share_rows, block_size), jnp.float32)
     for o in range(owners):
         for slot in range(capacity):
             at = o * capacity + slot
-            outgoing[o, pl.ds(slot * share_rows, share_rows)] = keep_ref[at] * partial[source_ref[at]]
+            outgoing[o, pl.ds(slot * share_rows, share_rows)] = partial[source_ref[at]]
     fourth = route(lambda p: outgoing.at[p], got_slots.at[here], route_sem, load_sem.at[3])
     for copies in (labels, fourth):
         arrived(copies)
@@ -124,7 +125,7 @@
             copy.wait_send()
 
 
-def term_stage(rights, lefts, psi_blocks, couplings, pattern, channel, source, keep, label_rows, channels):
+def term_stage(rights, lefts, psi_blocks, couplings, pattern, channel, source, label_rows, channels):
     sec_dev, block_size, _ = psi_blocks.shape
     n = couplings.shape[0]
     owners = label_rows.shape[0]
@@ -142,7 +143,7 @@
             jax.ShapeDtypeStruct(routed, jnp.float32),
             jax.ShapeDtypeStruct(label_rows.shape, jnp.float32),
         ),
-        in_specs=[hbm, hbm, hbm, smem, smem, smem, smem, smem, vmem],
+        in_specs=[hbm, hbm, hbm, smem, smem, smem, smem, vmem],
         out_specs=(vmem, vmem),
         scratch_shapes=[
             pltpu.VMEM(blocks, jnp.float32),
@@ -152,7 +153,7 @@
             pltpu.VMEM(blocks, jnp.float32),
             pltpu.VMEM(blocks, jnp.float32),
             pltpu.VMEM(tiles, jnp.float32),
-            pltpu.VMEM((sec_dev * channels, share_rows, block_size), jnp.float32),
+            pltpu.VMEM((sec_dev * channels + 1, share_rows, block_size), jnp.float32),
             pltpu.VMEM(routed, jnp.float32),
             pltpu.SemaphoreType.DMA((3, sec_dev, n)),
             pltpu.SemaphoreType.DMA((3, sec_dev, n)),
@@ -162,7 +163,7 @@
             pltpu.SemaphoreType.DMA((2, owners)),
         ],
         compiler_params=pltpu.CompilerParams(collective_id=0, has_side_effects=True),
-    )(rights, lefts, psi_blocks, couplings, pattern, channel, source, keep, label_rows)
+    )(rights, lefts, psi_blocks, couplings, pattern, channel, source, label_rows)
 
 
 def slot_tables(target, owners):
@@ -177,30 +178,31 @@
     buffer_rows = jnp.arange(owners * capacity, dtype=jnp.int32)
     placing = buffer_rows[:, None] == position[None, :]
     keep = jnp.any(placing, axis=1)
-    source = jnp.sum(jnp.where(placing, slot_order[None, :], 0), axis=1)
-    labels = jnp.sum(jnp.where(placing, (targets % sec_dev + 1)[None, :], 0), axis=1)
-    label_rows = jnp.zeros((owners, 1, 128), jnp.float32)
-    label_rows = label_rows.at[:, 0, :capacity].set(labels.reshape(owners, capacity).astype(jnp.float32))
-    return source.astype(jnp.int32), keep.astype(jnp.float32), label_rows
+    source = jnp.where(keep, jnp.sum(jnp.where(placing, slot_order[None, :], 0), axis=1), slot_count)
+    labels = jnp.sum(jnp.where(placing, (targets % sec_dev + 1)[None, :], 0), axis=1).astype(jnp.float32)
+    lanes = jnp.arange(128, dtype=jnp.int32)
+    label_rows = jnp.where(lanes[None, None, :] == jnp.arange(capacity, dtype=jnp.int32)[None, :, None],
+                           labels.reshape(owners, capacity)[:, :, None], 0.0)
+    label_rows = jnp.sum(label_rows, axis=1, keepdims=True)
+    return source.astype(jnp.int32), label_rows
 
 
 def pick_arrivals(got_slots, got_labels, sec_dev, capacity):
     owners, rows, block_size = got_slots.shape
     share_rows = rows // capacity
-    incoming = got_slots.reshape(owners * capacity, share_rows * block_size)
-    in_labels = got_labels[:, 0, :capacity].reshape(owners * capacity)
+    incoming = got_slots.reshape(owners, capacity, share_rows, block_size)
+    in_labels = got_labels[:, 0, :capacity]
     local_ids = (jnp.arange(sec_dev, dtype=jnp.int32) + 1).astype(jnp.float32)
-    picking = (in_labels[None, :] == local_ids[:, None]).astype(jnp.float32)
-    result = jnp.dot(picking, incoming, precision=PRECISE, preferred_element_type=jnp.float32)
-    return result.reshape(sec_dev, share_rows, block_size)
+    picking = (in_labels[None, :, :] == local_ids[:, None, None]).astype(jnp.float32)
+    return jnp.einsum("pos,osrk->prk", picking, incoming, precision=PRECISE)
 
 
 def local(psi_blocks, left_ops, right_ops, couplings, pattern, channel, target):
     sec_dev, channels = target.shape
     owners = lax.axis_size("sector")
-    source, keep, label_rows = slot_tables(target, owners)
+    source, label_rows = slot_tables(target, owners)
     got_slots, got_labels = term_stage(
-        right_ops[0], left_ops[0], psi_blocks, couplings, pattern, channel, source, keep, label_rows, channels
+        right_ops[0], left_ops[0], psi_blocks, couplings, pattern.T, channel, source, label_rows, channels
     )
     return pick_arrivals(got_slots, got_labels, sec_dev, source.shape[0] // owners)
 

time: 90.7 us -> 88.8 us (0.979)
  local copies, waits for them, and re-layouts: 5.32 us -> 2.34 us
  matrix products: 0.22 us -> 1.25 us
    unnamed x5 -> x0, local copies, waits for them, and re-layouts: 2.04 us -> none
    dot_general x1, matrix products: 0.22 us -> 1.25 us  [pick_arrivals(): return jnp.einsum('pos,osrk->prk', picking, incoming, precision=PRECISE)]
    reshape x1 -> x0, local copies, waits for them, and re-layouts: 1 us -> none  [pick_arrivals(): incoming = got_slots.reshape(owners * capacity, share_rows * block_size)]
where the time goes in v7:
time: 88.8 us; the launch traced here: 88.5 us
  Pallas kernels  83.2 us (94%)
  local copies, waits for them, and re-layouts  2.34 us (3%)
  other arithmetic  1.64 us (2%)
  matrix products  1.25 us (1%)
    pallas_call x1, Pallas kernels, term_stage(): pl.pallas_call(functools.partial(term_kernel, n, owners), out_shape=(jax....  83.2 us

profile of v7, /device:TPU:1, one launch (start us, length us, event | category | flops | bytes accessed | tf_op | source)
XLA Modules:
  0.0 88.5 jit_solution(13381100698413334631)
XLA Ops:
  0.0 0.8 reshape.124
  0.8 0.2 convert_reduce_fusion
  1.0 0.1 select_reduce_fusion.1
  1.1 0.1 fusion.1
  1.2 0.5 broadcast_select_fusion.source_ref
  1.7 0.1 convert_element_type.23
  1.8 0.1 copy.14
  1.9 0.7 select_reduce_fusion
  2.6 83.2 %shard_map.73 = (f32[32,16,128]{2,1,0:T(8,128)}, f32[32,1,128]{2,1,0:T(1,128)}) custom-call(f32[4,128,128]{2,1,0:T(8,128)} %bitcast.13, f32[4,128,128]{2,1,0:T(8,128)} %bitcast.14, f32[4,128,128]{2,1,0:T(8,128)} %psi_hbm.1, f32[16,16]{1,0:T(8,128)} %coup_ref.1, s32[4,16]{1,0:T(4,128)} %bitcast.19, s32[16]{0:T(128)} %channel_ref.1, ...), custom_call_target="tpu_custom_call" | custom-call | tf_op jit(solution)/shard_map/pallas_call | solution.py:140
  85.8 0.8 copy.15
  86.6 1.2 %convolution_bitcast_fusion = f32[4,8,128]{2,0,1:T(4,128)S(1)} fusion(f32[32,2,8,128]{3,2,1,0:T(8,128)} %bitcast.15, f32[32,2]{0,1:T(2,128)S(1)} %bitcast.18, f32[4]{0:T(128)S(1)} %add_convert_fusion), kind=kOutput, calls=%fused_computation | convolution fusion | flops 3145984 | bytes 278800 | tf_op jit(solution)/shard_map/pos,osrk->prk/dot_general | solution.py:197
  87.9 0.6 copy.17
  (5 shorter events, 0.0 us)

commit v8 on v7

--- a/solution.py
+++ b/solution.py
@@ -18,8 +18,8 @@
 
 def term_kernel(
     n, owners, r_ref, l_hbm, psi_hbm, coup_ref, pattern_ref, channel_ref, source_ref, label_ref,
-    got_slots, got_labels,
-    l_ref, psi_ref, got_right, comp_rows, comp, contrib, got_contrib, partial, outgoing,
+    out_ref,
+    got_slots, got_labels, l_ref, psi_ref, got_right, comp_rows, comp, contrib, got_contrib, partial, outgoing,
     send_sem, recv_sem, local_sem, load_sem, route_sem, label_sem,
 ):
     me = lax.axis_index("term")
@@ -120,6 +120,17 @@
     fourth = route(lambda p: outgoing.at[p], got_slots.at[here], route_sem, load_sem.at[3])
     for copies in (labels, fourth):
         arrived(copies)
+    totals = [None] * sec_dev
+    for o in range(owners):
+        label_row = got_labels[o]
+        for slot in range(capacity):
+            label = jnp.broadcast_to(label_row[:, slot:slot + 1], (share_rows, block_size))
+            rows = got_slots[o, pl.ds(slot * share_rows, share_rows)]
+            for p in range(sec_dev):
+                part = jnp.where(label == float(p + 1), rows, 0.0)
+                totals[p] = part if totals[p] is None else totals[p] + part
+    for p in range(sec_dev):
+        out_ref[p] = totals[p]
     for copies in first + second + third + [labels, fourth]:
         for copy in copies[1:]:
             copy.wait_send()
@@ -139,13 +150,12 @@
     vmem = pl.BlockSpec(memory_space=pltpu.VMEM)
     return pl.pallas_call(
         functools.partial(term_kernel, n, owners),
-        out_shape=(
-            jax.ShapeDtypeStruct(routed, jnp.float32),
-            jax.ShapeDtypeStruct(label_rows.shape, jnp.float32),
-        ),
+        out_shape=jax.ShapeDtypeStruct((sec_dev, share_rows, block_size), jnp.float32),
         in_specs=[hbm, hbm, hbm, smem, smem, smem, smem, vmem],
-        out_specs=(vmem, vmem),
+        out_specs=vmem,
         scratch_shapes=[
+            pltpu.VMEM(routed, jnp.float32),
+            pltpu.VMEM(label_rows.shape, jnp.float32),
             pltpu.VMEM(blocks, jnp.float32),
             pltpu.VMEM(blocks, jnp.float32),
             pltpu.VMEM(tiles, jnp.float32),
@@ -187,24 +197,13 @@
     return source.astype(jnp.int32), label_rows
 
 
-def pick_arrivals(got_slots, got_labels, sec_dev, capacity):
-    owners, rows, block_size = got_slots.shape
-    share_rows = rows // capacity
-    incoming = got_slots.reshape(owners, capacity, share_rows, block_size)
-    in_labels = got_labels[:, 0, :capacity]
-    local_ids = (jnp.arange(sec_dev, dtype=jnp.int32) + 1).astype(jnp.float32)
-    picking = (in_labels[None, :, :] == local_ids[:, None, None]).astype(jnp.float32)
-    return jnp.einsum("pos,osrk->prk", picking, incoming, precision=PRECISE)
-
-
 def local(psi_blocks, left_ops, right_ops, couplings, pattern, channel, target):
     sec_dev, channels = target.shape
     owners = lax.axis_size("sector")
     source, label_rows = slot_tables(target, owners)
-    got_slots, got_labels = term_stage(
+    return term_stage(
         right_ops[0], left_ops[0], psi_blocks, couplings, pattern.T, channel, source, label_rows, channels
     )
-    return pick_arrivals(got_slots, got_labels, sec_dev, source.shape[0] // owners)
 
 
 def solution(mesh):

time: 88.8 us -> 87.4 us (0.984)
  matrix products: 1.25 us -> 0 us
    unnamed x0 -> x3, local copies, waits for them, and re-layouts: none -> 2.01 us
    dot_general x1 -> x0, matrix products: 1.25 us -> none  [pick_arrivals(): return jnp.einsum('pos,osrk->prk', picking, incoming, precision=PRECISE)]
where the time goes in v8:
time: 87.4 us; the launch traced here: 87.2 us
  Pallas kernels  83.3 us (95%)
  local copies, waits for them, and re-layouts  2.26 us (3%)
  other arithmetic  1.6 us (2%)
    pallas_call x1, Pallas kernels, term_stage(): pl.pallas_call(functools.partial(term_kernel, n, owners), out_shape=jax.S...  83.3 us
    unnamed x3, local copies, waits for them, and re-layouts  2.01 us

profile of v8, /device:TPU:1, one launch (start us, length us, event | category | flops | bytes accessed | tf_op | source)
XLA Modules:
  0.0 87.2 jit_solution(4300092304159069884)
XLA Ops:
  0.0 0.0 copy-start
  0.0 0.7 copy-done
  0.7 0.1 reshape.115
  0.8 0.2 convert_reduce_fusion
  1.0 0.1 fusion
  1.1 0.1 select_reduce_fusion.1
  1.2 0.5 broadcast_select_fusion.source_ref
  1.7 0.1 convert_element_type.15
  1.8 0.1 copy.8
  1.9 0.7 select_reduce_fusion
  2.6 83.3 %shard_map.73 = f32[4,8,128]{2,1,0:T(8,128)} custom-call(f32[4,128,128]{2,1,0:T(8,128)} %bitcast.4, f32[4,128,128]{2,1,0:T(8,128)} %bitcast.5, f32[4,128,128]{2,1,0:T(8,128)} %psi_hbm.1, f32[16,16]{1,0:T(8,128)} %coup_ref.1, s32[4,16]{1,0:T(4,128)} %bitcast.7, s32[16]{0:T(128)} %channel_ref.1, s32[64]{0:T(128)} %broadcast_select_fusion.source_ref, ...), custom_call_target="tpu_custom_call" | custom-call | tf_op jit(solution)/shard_map/pallas_call | solution.py:151
  85.8 1.3 %copy.10 = f32[4,8,128]{2,1,0:T(8,128)} copy(f32[4,8,128]{2,1,0:T(8,128)} %shard_map.73) | data formatting | bytes 32768
  (4 shorter events, 0.0 us)
Async XLA Ops:
  0.0 0.7 copy-start

commit v9 on v8

--- a/solution.py
+++ b/solution.py
@@ -26,7 +26,7 @@
     here = lax.axis_index("sector")
     sec_dev, _, share_rows, block_size = got_right.shape
     channels = (partial.shape[0] - 1) // sec_dev
-    capacity = outgoing.shape[1] // share_rows
+    capacity = outgoing.shape[2] // (share_rows // 2)
     barrier = pltpu.get_barrier_semaphore()
     for k in range(1, n):
         pl.semaphore_signal(barrier, inc=1, device_id={"term": lax.rem(me + k, n)}, device_id_type=MESH)
@@ -96,42 +96,49 @@
         second.append(send(1, s, lambda p, s=s: comp_rows.at[s, p], comp.at[s, rows_of(me, share_rows)]))
     for load in loads:
         load.wait()
-    third = []
+    half = share_rows // 2
+    third = [[], []]
     for s in range(sec_dev):
         arrived(second[s])
         inner = jnp.dot(psi_ref[s], comp[s], precision=PRECISE, preferred_element_type=jnp.float32)
         contrib[s] = jnp.dot(l_ref[s], inner, precision=PRECISE, preferred_element_type=jnp.float32)
-        third.append(send(2, s, lambda p, s=s: contrib.at[s, rows_of(p, share_rows)], got_contrib.at[s, me]))
+        third[0].append(send(2, s, lambda p, s=s: contrib.at[s, pl.ds(p * share_rows, half)], got_contrib.at[s, me, pl.ds(0, half)]))
     for s in range(sec_dev):
-        arrived(third[s])
-        parts = [gathered(got_contrib, s, k) for k in range(n)]
-        for c in range(channels):
-            total = None
-            for k in range(n):
-                term = lax.rem(me + k, n)
-                live = jnp.where(channel_ref[term] == c, pattern_ref[s, term], 0).astype(jnp.float32)
-                total = live * parts[k] if total is None else total + live * parts[k]
-            partial[s * channels + c] = total
+        third[1].append(send(3, s, lambda p, s=s: contrib.at[s, pl.ds(p * share_rows + half, half)], got_contrib.at[s, me, pl.ds(half, half)]))
     partial[sec_dev * channels] = jnp.zeros((share_rows, block_size), jnp.float32)
-    for o in range(owners):
-        for slot in range(capacity):
-            at = o * capacity + slot
-            outgoing[o, pl.ds(slot * share_rows, share_rows)] = partial[source_ref[at]]
-    fourth = route(lambda p: outgoing.at[p], got_slots.at[here], route_sem, load_sem.at[3])
-    for copies in (labels, fourth):
-        arrived(copies)
-    totals = [None] * sec_dev
-    for o in range(owners):
-        label_row = got_labels[o]
-        for slot in range(capacity):
-            label = jnp.broadcast_to(label_row[:, slot:slot + 1], (share_rows, block_size))
-            rows = got_slots[o, pl.ds(slot * share_rows, share_rows)]
-            for p in range(sec_dev):
-                part = jnp.where(label == float(p + 1), rows, 0.0)
-                totals[p] = part if totals[p] is None else totals[p] + part
-    for p in range(sec_dev):
-        out_ref[p] = totals[p]
-    for copies in first + second + third + [labels, fourth]:
+    fourth = []
+    for h in range(2):
+        rows_h = pl.ds(h * half, half)
+        for s in range(sec_dev):
+            arrived(third[h][s])
+            parts = [got_contrib[s, lax.rem(me + k, n), rows_h] for k in range(n)]
+            for c in range(channels):
+                total = None
+                for k in range(n):
+                    term = lax.rem(me + k, n)
+                    live = jnp.where(channel_ref[term] == c, pattern_ref[s, term], 0).astype(jnp.float32)
+                    total = live * parts[k] if total is None else total + live * parts[k]
+                partial[s * channels + c, rows_h] = total
+        for o in range(owners):
+            for slot in range(capacity):
+                at = o * capacity + slot
+                outgoing[h, o, pl.ds(slot * half, half)] = partial[source_ref[at], rows_h]
+        fourth.append(route(lambda p, h=h: outgoing.at[h, p], got_slots.at[h, here], route_sem.at[h], load_sem.at[3 + h]))
+    arrived(labels)
+    for h in range(2):
+        arrived(fourth[h])
+        totals = [None] * sec_dev
+        for o in range(owners):
+            label_row = got_labels[o]
+            for slot in range(capacity):
+                label = jnp.broadcast_to(label_row[:, slot:slot + 1], (half, block_size))
+                rows = got_slots[h, o, pl.ds(slot * half, half)]
+                for p in range(sec_dev):
+                    part = jnp.where(label == float(p + 1), rows, 0.0)
+                    totals[p] = part if totals[p] is None else totals[p] + part
+        for p in range(sec_dev):
+            out_ref[p, pl.ds(h * half, half)] = totals[p]
+    for copies in first + second + third[0] + third[1] + [labels] + fourth:
         for copy in copies[1:]:
             copy.wait_send()
 
@@ -144,7 +151,7 @@
     share_rows = block_size // n
     tiles = (sec_dev, n, share_rows, block_size)
     blocks = (sec_dev, block_size, block_size)
-    routed = (owners, capacity * share_rows, block_size)
+    routed = (owners, capacity * share_rows // 2, block_size)
     hbm = pl.BlockSpec(memory_space=pl.ANY)
     smem = pl.BlockSpec(memory_space=pltpu.SMEM)
     vmem = pl.BlockSpec(memory_space=pltpu.VMEM)
@@ -154,7 +161,7 @@
         in_specs=[hbm, hbm, hbm, smem, smem, smem, smem, vmem],
         out_specs=vmem,
         scratch_shapes=[
-            pltpu.VMEM(routed, jnp.float32),
+            pltpu.VMEM((2,) + routed, jnp.float32),
             pltpu.VMEM(label_rows.shape, jnp.float32),
             pltpu.VMEM(blocks, jnp.float32),
             pltpu.VMEM(blocks, jnp.float32),
@@ -164,12 +171,12 @@
             pltpu.VMEM(blocks, jnp.float32),
             pltpu.VMEM(tiles, jnp.float32),
             pltpu.VMEM((sec_dev * channels + 1, share_rows, block_size), jnp.float32),
-            pltpu.VMEM(routed, jnp.float32),
-            pltpu.SemaphoreType.DMA((3, sec_dev, n)),
-            pltpu.SemaphoreType.DMA((3, sec_dev, n)),
-            pltpu.SemaphoreType.DMA((3, sec_dev)),
-            pltpu.SemaphoreType.DMA((4,)),
-            pltpu.SemaphoreType.DMA((2, owners)),
+            pltpu.VMEM((2,) + routed, jnp.float32),
+            pltpu.SemaphoreType.DMA((4, sec_dev, n)),
+            pltpu.SemaphoreType.DMA((4, sec_dev, n)),
+            pltpu.SemaphoreType.DMA((4, sec_dev)),
+            pltpu.SemaphoreType.DMA((5,)),
+            pltpu.SemaphoreType.DMA((2, 2, owners)),
             pltpu.SemaphoreType.DMA((2, owners)),
         ],
         compiler_params=pltpu.CompilerParams(collective_id=0, has_side_effects=True),

time: 87.4 us -> 89.4 us (1.023)
  Pallas kernels: 83.3 us -> 85.2 us
    pallas_call x1, Pallas kernels: 83.3 us -> 85.2 us  [term_stage(): pl.pallas_call(functools.partial(term_kernel, n, owners), out_shape=jax.S...]
where the time goes in v9:
time: 89.4 us; the launch traced here: 89.1 us
  Pallas kernels  85.2 us (95%)
  local copies, waits for them, and re-layouts  2.26 us (3%)
  other arithmetic  1.6 us (2%)
    pallas_call x1, Pallas kernels, term_stage(): pl.pallas_call(functools.partial(term_kernel, n, owners), out_shape=jax.S...  85.2 us
    unnamed x3, local copies, waits for them, and re-layouts  2.01 us

profile of v9, /device:TPU:1, one launch (start us, length us, event | category | flops | bytes accessed | tf_op | source)
XLA Modules:
  0.0 89.1 jit_solution(7075829146781234035)
XLA Ops:
  0.0 0.0 copy-start
  0.0 0.7 copy-done
  0.7 0.1 reshape.115
  0.8 0.2 convert_reduce_fusion
  1.0 0.1 fusion
  1.1 0.1 select_reduce_fusion.1
  1.2 0.5 broadcast_select_fusion.source_ref
  1.7 0.1 convert_element_type.15
  1.8 0.1 copy.8
  1.9 0.7 select_reduce_fusion
  2.6 85.2 %shard_map.73 = f32[4,8,128]{2,1,0:T(8,128)} custom-call(f32[4,128,128]{2,1,0:T(8,128)} %bitcast.4, f32[4,128,128]{2,1,0:T(8,128)} %bitcast.5, f32[4,128,128]{2,1,0:T(8,128)} %psi_hbm.1, f32[16,16]{1,0:T(8,128)} %coup_ref.1, s32[4,16]{1,0:T(4,128)} %bitcast.7, s32[16]{0:T(128)} %channel_ref.1, s32[64]{0:T(128)} %broadcast_select_fusion.source_ref, ...), custom_call_target="tpu_custom_call" | custom-call | tf_op jit(solution)/shard_map/pallas_call | solution.py:158
  87.8 1.3 %copy.10 = f32[4,8,128]{2,1,0:T(8,128)} copy(f32[4,8,128]{2,1,0:T(8,128)} %shard_map.73) | data formatting | bytes 32768
  (4 shorter events, 0.0 us)
Async XLA Ops:
  0.0 0.7 copy-start

commit v10 on v8

--- a/solution.py
+++ b/solution.py
@@ -17,9 +17,9 @@
 
 
 def term_kernel(
-    n, owners, r_ref, l_hbm, psi_hbm, coup_ref, pattern_ref, channel_ref, source_ref, label_ref,
+    n, owners, r_ref, l_hbm, psi_hbm, coup_ref, pattern_ref, channel_ref, target_ref,
     out_ref,
-    got_slots, got_labels, l_ref, psi_ref, got_right, comp_rows, comp, contrib, got_contrib, partial, outgoing,
+    got_slots, got_labels, label_rows, key_tab, label_tab, source_tab, slot_label, l_ref, psi_ref, got_right, comp_rows, comp, contrib, got_contrib, partial, outgoing,
     send_sem, recv_sem, local_sem, load_sem, route_sem, label_sem,
 ):
     me = lax.axis_index("term")
@@ -52,7 +52,6 @@
             copies.append(copy)
         return copies
 
-    labels = route(lambda p: label_ref.at[p], got_labels.at[here], label_sem, load_sem.at[2])
 
     def send(stage, s, src_of, dst):
         local = pltpu.make_async_copy(src_of(me), dst, local_sem.at[stage, s])
@@ -84,6 +83,39 @@
     for load in loads:
         load.start()
     first = [send(0, s, lambda p, s=s: r_ref.at[s, rows_of(p, share_rows)], got_right.at[s, me]) for s in range(sec_dev)]
+    slot_count = sec_dev * channels
+    owner_of = [target_ref[i // channels, i % channels] // sec_dev for i in range(slot_count)]
+    for i in range(slot_count):
+        rank = 0
+        for j in range(i):
+            rank = rank + jnp.where(owner_of[j] == owner_of[i], 1, 0)
+        key_tab[i] = owner_of[i] * capacity + rank
+        label_tab[i] = (target_ref[i // channels, i % channels] % sec_dev + 1).astype(jnp.float32)
+
+    def fill_row(q, carry):
+        found = jnp.int32(slot_count)
+        label = jnp.float32(0.0)
+        for i in range(slot_count):
+            hit = key_tab[i] == q
+            found = jnp.where(hit, i, found)
+            label = jnp.where(hit, label_tab[i], label)
+        source_tab[q] = found
+        slot_label[q] = label
+        return carry
+
+    lax.fori_loop(0, owners * capacity, fill_row, 0)
+    lanes = lax.broadcasted_iota(jnp.int32, (1, block_size), 1)
+
+    def fill_labels(o, carry):
+        row = jnp.zeros((1, block_size), jnp.float32)
+        for slot in range(capacity):
+            row = jnp.where(lanes == slot, slot_label[o * capacity + slot], row)
+        label_rows[o] = row
+        return carry
+
+    lax.fori_loop(0, owners, fill_labels, 0)
+    labels = route(lambda p: label_rows.at[p], got_labels.at[here], label_sem, load_sem.at[2])
+
     second = []
     for s in range(sec_dev):
         arrived(first[s])
@@ -116,7 +148,7 @@
     for o in range(owners):
         for slot in range(capacity):
             at = o * capacity + slot
-            outgoing[o, pl.ds(slot * share_rows, share_rows)] = partial[source_ref[at]]
+            outgoing[o, pl.ds(slot * share_rows, share_rows)] = partial[source_tab[at]]
     fourth = route(lambda p: outgoing.at[p], got_slots.at[here], route_sem, load_sem.at[3])
     for copies in (labels, fourth):
         arrived(copies)
@@ -136,11 +168,11 @@
             copy.wait_send()
 
 
-def term_stage(rights, lefts, psi_blocks, couplings, pattern, channel, source, label_rows, channels):
+def term_stage(rights, lefts, psi_blocks, couplings, pattern, channel, target, owners):
     sec_dev, block_size, _ = psi_blocks.shape
     n = couplings.shape[0]
-    owners = label_rows.shape[0]
-    capacity = source.shape[0] // owners
+    channels = target.shape[1]
+    capacity = max(2, (sec_dev * channels + owners - 1) // owners)
     share_rows = block_size // n
     tiles = (sec_dev, n, share_rows, block_size)
     blocks = (sec_dev, block_size, block_size)
@@ -151,11 +183,16 @@
     return pl.pallas_call(
         functools.partial(term_kernel, n, owners),
         out_shape=jax.ShapeDtypeStruct((sec_dev, share_rows, block_size), jnp.float32),
-        in_specs=[hbm, hbm, hbm, smem, smem, smem, smem, vmem],
+        in_specs=[hbm, hbm, hbm, smem, smem, smem, smem],
         out_specs=vmem,
         scratch_shapes=[
             pltpu.VMEM(routed, jnp.float32),
-            pltpu.VMEM(label_rows.shape, jnp.float32),
+            pltpu.VMEM((owners, 1, block_size), jnp.float32),
+            pltpu.VMEM((owners, 1, block_size), jnp.float32),
+            pltpu.SMEM((sec_dev * channels,), jnp.int32),
+            pltpu.SMEM((sec_dev * channels,), jnp.float32),
+            pltpu.SMEM((owners * capacity,), jnp.int32),
+            pltpu.SMEM((owners * capacity,), jnp.float32),
             pltpu.VMEM(blocks, jnp.float32),
             pltpu.VMEM(blocks, jnp.float32),
             pltpu.VMEM(tiles, jnp.float32),
@@ -173,37 +210,12 @@
             pltpu.SemaphoreType.DMA((2, owners)),
         ],
         compiler_params=pltpu.CompilerParams(collective_id=0, has_side_effects=True),
-    )(rights, lefts, psi_blocks, couplings, pattern, channel, source, label_rows)
-
-
-def slot_tables(target, owners):
-    sec_dev, channels = target.shape
-    slot_count = sec_dev * channels
-    targets = target.reshape(slot_count)
-    capacity = max(2, (slot_count + owners - 1) // owners)
-    destination = targets // sec_dev
-    slot_order = jnp.arange(slot_count, dtype=jnp.int32)
-    earlier = (destination[None, :] == destination[:, None]) & (slot_order[None, :] < slot_order[:, None])
-    position = destination * capacity + jnp.sum(earlier.astype(jnp.int32), axis=1)
-    buffer_rows = jnp.arange(owners * capacity, dtype=jnp.int32)
-    placing = buffer_rows[:, None] == position[None, :]
-    keep = jnp.any(placing, axis=1)
-    source = jnp.where(keep, jnp.sum(jnp.where(placing, slot_order[None, :], 0), axis=1), slot_count)
-    labels = jnp.sum(jnp.where(placing, (targets % sec_dev + 1)[None, :], 0), axis=1).astype(jnp.float32)
-    lanes = jnp.arange(128, dtype=jnp.int32)
-    label_rows = jnp.where(lanes[None, None, :] == jnp.arange(capacity, dtype=jnp.int32)[None, :, None],
-                           labels.reshape(owners, capacity)[:, :, None], 0.0)
-    label_rows = jnp.sum(label_rows, axis=1, keepdims=True)
-    return source.astype(jnp.int32), label_rows
+    )(rights, lefts, psi_blocks, couplings, pattern, channel, target)
 
 
 def local(psi_blocks, left_ops, right_ops, couplings, pattern, channel, target):
-    sec_dev, channels = target.shape
     owners = lax.axis_size("sector")
-    source, label_rows = slot_tables(target, owners)
-    return term_stage(
-        right_ops[0], left_ops[0], psi_blocks, couplings, pattern.T, channel, source, label_rows, channels
-    )
+    return term_stage(right_ops[0], left_ops[0], psi_blocks, couplings, pattern.T, channel, target, owners)
 
 
 def solution(mesh):

time: 87.4 us -> 84.3 us (0.965)
  the two profiles are of different devices: /device:TPU:1 before, /device:TPU:6 now
where the time goes in v10:
time: 84.3 us; the launch traced here: 84.1 us
  Pallas kernels  82.8 us (98%)
  local copies, waits for them, and re-layouts  1.32 us (2%)
    pallas_call x1, Pallas kernels, term_stage(): pl.pallas_call(functools.partial(term_kernel, n, owners), out_shape=jax.S...  82.8 us

profile of v10, /device:TPU:6, one launch (start us, length us, event | category | flops | bytes accessed | tf_op | source)
XLA Modules:
  0.0 84.1 jit_solution(2543505715022864702)
XLA Ops:
  0.0 82.8 %shard_map.73 = f32[4,8,128]{2,1,0:T(8,128)} custom-call(f32[4,128,128]{2,1,0:T(8,128)} %bitcast.3, f32[4,128,128]{2,1,0:T(8,128)} %bitcast.4, f32[4,128,128]{2,1,0:T(8,128)} %psi_hbm.1, f32[16,16]{1,0:T(8,128)} %coup_ref.1, s32[4,16]{1,0:T(4,128)} %bitcast.5, s32[16]{0:T(128)} %channel_ref.1, s32[4,8]{1,0:T(4,128)} %target_ref.1), custom_call_target="tpu_custom_call" | custom-call | tf_op jit(solution)/shard_map/pallas_call | solution.py:183
  82.8 1.3 %copy.9 = f32[4,8,128]{2,1,0:T(8,128)} copy(f32[4,8,128]{2,1,0:T(8,128)} %shard_map.73) | data formatting | bytes 32768

commit v11 on v10

--- a/solution.py
+++ b/solution.py
@@ -27,6 +27,9 @@
     sec_dev, _, share_rows, block_size = got_right.shape
     channels = (partial.shape[0] - 1) // sec_dev
     capacity = outgoing.shape[1] // share_rows
+    loads = [pltpu.make_async_copy(l_hbm, l_ref, load_sem.at[0]), pltpu.make_async_copy(psi_hbm, psi_ref, load_sem.at[1])]
+    for load in loads:
+        load.start()
     barrier = pltpu.get_barrier_semaphore()
     for k in range(1, n):
         pl.semaphore_signal(barrier, inc=1, device_id={"term": lax.rem(me + k, n)}, device_id_type=MESH)
@@ -79,9 +82,6 @@
     def gathered(buf, s, k):
         return buf[s, lax.rem(me + k, n)]
 
-    loads = [pltpu.make_async_copy(l_hbm, l_ref, load_sem.at[0]), pltpu.make_async_copy(psi_hbm, psi_ref, load_sem.at[1])]
-    for load in loads:
-        load.start()
     first = [send(0, s, lambda p, s=s: r_ref.at[s, rows_of(p, share_rows)], got_right.at[s, me]) for s in range(sec_dev)]
     slot_count = sec_dev * channels
     owner_of = [target_ref[i // channels, i % channels] // sec_dev for i in range(slot_count)]
@@ -115,6 +115,10 @@
 
     lax.fori_loop(0, owners, fill_labels, 0)
     labels = route(lambda p: label_rows.at[p], got_labels.at[here], label_sem, load_sem.at[2])
+    for load in loads:
+        load.wait()
+    for s in range(sec_dev):
+        l_ref[s] = jnp.dot(l_ref[s], psi_ref[s], precision=PRECISE, preferred_element_type=jnp.float32)
 
     second = []
     for s in range(sec_dev):
@@ -126,13 +130,10 @@
                 total = total + coup_ref[a, lax.rem(me + k, n)] * parts[k]
             comp_rows[s, a] = total
         second.append(send(1, s, lambda p, s=s: comp_rows.at[s, p], comp.at[s, rows_of(me, share_rows)]))
-    for load in loads:
-        load.wait()
     third = []
     for s in range(sec_dev):
         arrived(second[s])
-        inner = jnp.dot(psi_ref[s], comp[s], precision=PRECISE, preferred_element_type=jnp.float32)
-        contrib[s] = jnp.dot(l_ref[s], inner, precision=PRECISE, preferred_element_type=jnp.float32)
+        contrib[s] = jnp.dot(l_ref[s], comp[s], precision=PRECISE, preferred_element_type=jnp.float32)
         third.append(send(2, s, lambda p, s=s: contrib.at[s, rows_of(p, share_rows)], got_contrib.at[s, me]))
     for s in range(sec_dev):
         arrived(third[s])

time: 84.3 us -> 84.2 us (level)
  the two profiles are of different devices: /device:TPU:6 before, /device:TPU:1 now
where the time goes in v11:
time: 84.2 us; the launch traced here: 84 us
  Pallas kernels  82.7 us (98%)
  local copies, waits for them, and re-layouts  1.32 us (2%)
    pallas_call x1, Pallas kernels, term_stage(): pl.pallas_call(functools.partial(term_kernel, n, owners), out_shape=jax.S...  82.7 us

profile of v11, /device:TPU:1, one launch (start us, length us, event | category | flops | bytes accessed | tf_op | source)
XLA Modules:
  0.0 84.0 jit_solution(15572532961614169543)
XLA Ops:
  0.0 82.7 %shard_map.73 = f32[4,8,128]{2,1,0:T(8,128)} custom-call(f32[4,128,128]{2,1,0:T(8,128)} %bitcast.3, f32[4,128,128]{2,1,0:T(8,128)} %bitcast.4, f32[4,128,128]{2,1,0:T(8,128)} %psi_hbm.1, f32[16,16]{1,0:T(8,128)} %coup_ref.1, s32[4,16]{1,0:T(4,128)} %bitcast.5, s32[16]{0:T(128)} %channel_ref.1, s32[4,8]{1,0:T(4,128)} %target_ref.1), custom_call_target="tpu_custom_call" | custom-call | tf_op jit(solution)/shard_map/pallas_call | solution.py:184
  82.7 1.3 %copy.9 = f32[4,8,128]{2,1,0:T(8,128)} copy(f32[4,8,128]{2,1,0:T(8,128)} %shard_map.73) | data formatting | bytes 32768

commit v12 on v11

--- a/solution.py
+++ b/solution.py
@@ -136,14 +136,17 @@
         contrib[s] = jnp.dot(l_ref[s], comp[s], precision=PRECISE, preferred_element_type=jnp.float32)
         third.append(send(2, s, lambda p, s=s: contrib.at[s, rows_of(p, share_rows)], got_contrib.at[s, me]))
     for s in range(sec_dev):
+        terms = [lax.rem(me + k, n) for k in range(n)]
+        lives = [
+            [jnp.where(channel_ref[terms[k]] == c, pattern_ref[s, terms[k]], 0).astype(jnp.float32) for k in range(n)]
+            for c in range(channels)
+        ]
         arrived(third[s])
         parts = [gathered(got_contrib, s, k) for k in range(n)]
         for c in range(channels):
-            total = None
-            for k in range(n):
-                term = lax.rem(me + k, n)
-                live = jnp.where(channel_ref[term] == c, pattern_ref[s, term], 0).astype(jnp.float32)
-                total = live * parts[k] if total is None else total + live * parts[k]
+            total = lives[c][0] * parts[0]
+            for k in range(1, n):
+                total = total + lives[c][k] * parts[k]
             partial[s * channels + c] = total
     partial[sec_dev * channels] = jnp.zeros((share_rows, block_size), jnp.float32)
     for o in range(owners):
@@ -151,10 +154,14 @@
             at = o * capacity + slot
             outgoing[o, pl.ds(slot * share_rows, share_rows)] = partial[source_tab[at]]
     fourth = route(lambda p: outgoing.at[p], got_slots.at[here], route_sem, load_sem.at[3])
-    for copies in (labels, fourth):
-        arrived(copies)
+    arrived(labels)
     totals = [None] * sec_dev
-    for o in range(owners):
+    for k in range(owners):
+        if k == 0:
+            fourth[0].wait()
+        else:
+            fourth[k].wait_recv()
+        o = lax.rem(here + owners - k, owners)
         label_row = got_labels[o]
         for slot in range(capacity):
             label = jnp.broadcast_to(label_row[:, slot:slot + 1], (share_rows, block_size))

time: 84.2 us -> 84.8 us (level)
  no operation moved by 1% of the time
where the time goes in v12:
time: 84.8 us; the launch traced here: 84.6 us
  Pallas kernels  83.3 us (98%)
  local copies, waits for them, and re-layouts  1.32 us (2%)
    pallas_call x1, Pallas kernels, term_stage(): pl.pallas_call(functools.partial(term_kernel, n, owners), out_shape=jax.S...  83.3 us

profile of v12, /device:TPU:1, one launch (start us, length us, event | category | flops | bytes accessed | tf_op | source)
XLA Modules:
  0.0 84.6 jit_solution(6832005412338464391)
XLA Ops:
  0.0 83.3 %shard_map.73 = f32[4,8,128]{2,1,0:T(8,128)} custom-call(f32[4,128,128]{2,1,0:T(8,128)} %bitcast.3, f32[4,128,128]{2,1,0:T(8,128)} %bitcast.4, f32[4,128,128]{2,1,0:T(8,128)} %psi_hbm.1, f32[16,16]{1,0:T(8,128)} %coup_ref.1, s32[4,16]{1,0:T(4,128)} %bitcast.5, s32[16]{0:T(128)} %channel_ref.1, s32[4,8]{1,0:T(4,128)} %target_ref.1), custom_call_target="tpu_custom_call" | custom-call | tf_op jit(solution)/shard_map/pallas_call | solution.py:191
  83.3 1.3 %copy.9 = f32[4,8,128]{2,1,0:T(8,128)} copy(f32[4,8,128]{2,1,0:T(8,128)} %shard_map.73) | data formatting | bytes 32768

commit v13 on v11

--- a/solution.py
+++ b/solution.py
@@ -19,7 +19,7 @@
 def term_kernel(
     n, owners, r_ref, l_hbm, psi_hbm, coup_ref, pattern_ref, channel_ref, target_ref,
     out_ref,
-    got_slots, got_labels, label_rows, key_tab, label_tab, source_tab, slot_label, l_ref, psi_ref, got_right, comp_rows, comp, contrib, got_contrib, partial, outgoing,
+    got_slots, got_labels, label_rows, key_tab, label_tab, source_tab, slot_label, r_vmem, l_ref, psi_ref, got_right, comp_rows, comp, contrib, got_contrib, partial, outgoing,
     send_sem, recv_sem, local_sem, load_sem, route_sem, label_sem,
 ):
     me = lax.axis_index("term")
@@ -27,6 +27,8 @@
     sec_dev, _, share_rows, block_size = got_right.shape
     channels = (partial.shape[0] - 1) // sec_dev
     capacity = outgoing.shape[1] // share_rows
+    right_load = pltpu.make_async_copy(r_ref, r_vmem, load_sem.at[4])
+    right_load.start()
     loads = [pltpu.make_async_copy(l_hbm, l_ref, load_sem.at[0]), pltpu.make_async_copy(psi_hbm, psi_ref, load_sem.at[1])]
     for load in loads:
         load.start()
@@ -82,7 +84,8 @@
     def gathered(buf, s, k):
         return buf[s, lax.rem(me + k, n)]
 
-    first = [send(0, s, lambda p, s=s: r_ref.at[s, rows_of(p, share_rows)], got_right.at[s, me]) for s in range(sec_dev)]
+    right_load.wait()
+    first = [send(0, s, lambda p, s=s: r_vmem.at[s, rows_of(p, share_rows)], got_right.at[s, me]) for s in range(sec_dev)]
     slot_count = sec_dev * channels
     owner_of = [target_ref[i // channels, i % channels] // sec_dev for i in range(slot_count)]
     for i in range(slot_count):
@@ -196,6 +199,7 @@
             pltpu.SMEM((owners * capacity,), jnp.float32),
             pltpu.VMEM(blocks, jnp.float32),
             pltpu.VMEM(blocks, jnp.float32),
+            pltpu.VMEM(blocks, jnp.float32),
             pltpu.VMEM(tiles, jnp.float32),
             pltpu.VMEM(tiles, jnp.float32),
             pltpu.VMEM(blocks, jnp.float32),
@@ -206,7 +210,7 @@
             pltpu.SemaphoreType.DMA((3, sec_dev, n)),
             pltpu.SemaphoreType.DMA((3, sec_dev, n)),
             pltpu.SemaphoreType.DMA((3, sec_dev)),
-            pltpu.SemaphoreType.DMA((4,)),
+            pltpu.SemaphoreType.DMA((5,)),
             pltpu.SemaphoreType.DMA((2, owners)),
             pltpu.SemaphoreType.DMA((2, owners)),
         ],

time: 84.2 us -> 84.1 us (level)
  no operation moved by 1% of the time
where the time goes in v13:
time: 84.1 us; the launch traced here: 83.9 us
  Pallas kernels  82.5 us (98%)
  local copies, waits for them, and re-layouts  1.32 us (2%)
    pallas_call x1, Pallas kernels, term_stage(): pl.pallas_call(functools.partial(term_kernel, n, owners), out_shape=jax.S...  82.5 us

profile of v13, /device:TPU:1, one launch (start us, length us, event | category | flops | bytes accessed | tf_op | source)
XLA Modules:
  0.0 83.9 jit_solution(18067228162741159940)
XLA Ops:
  0.0 82.5 %shard_map.73 = f32[4,8,128]{2,1,0:T(8,128)} custom-call(f32[4,128,128]{2,1,0:T(8,128)} %bitcast.3, f32[4,128,128]{2,1,0:T(8,128)} %bitcast.4, f32[4,128,128]{2,1,0:T(8,128)} %psi_hbm.1, f32[16,16]{1,0:T(8,128)} %coup_ref.1, s32[4,16]{1,0:T(4,128)} %bitcast.5, s32[16]{0:T(128)} %channel_ref.1, s32[4,8]{1,0:T(4,128)} %target_ref.1), custom_call_target="tpu_custom_call" | custom-call | tf_op jit(solution)/shard_map/pallas_call | solution.py:187
  82.5 1.3 %copy.9 = f32[4,8,128]{2,1,0:T(8,128)} copy(f32[4,8,128]{2,1,0:T(8,128)} %shard_map.73) | data formatting | bytes 32768

commit v14 on v11

--- a/solution.py
+++ b/solution.py
@@ -83,6 +83,26 @@
         return buf[s, lax.rem(me + k, n)]
 
     first = [send(0, s, lambda p, s=s: r_ref.at[s, rows_of(p, share_rows)], got_right.at[s, me]) for s in range(sec_dev)]
+    for load in loads:
+        load.wait()
+    for s in range(sec_dev):
+        l_ref[s] = jnp.dot(l_ref[s], psi_ref[s], precision=PRECISE, preferred_element_type=jnp.float32)
+
+    second = []
+    for s in range(sec_dev):
+        arrived(first[s])
+        parts = [gathered(got_right, s, k) for k in range(n)]
+        for a in range(n):
+            total = coup_ref[a, me] * parts[0]
+            for k in range(1, n):
+                total = total + coup_ref[a, lax.rem(me + k, n)] * parts[k]
+            comp_rows[s, a] = total
+        second.append(send(1, s, lambda p, s=s: comp_rows.at[s, p], comp.at[s, rows_of(me, share_rows)]))
+    third = []
+    for s in range(sec_dev):
+        arrived(second[s])
+        contrib[s] = jnp.dot(l_ref[s], comp[s], precision=PRECISE, preferred_element_type=jnp.float32)
+        third.append(send(2, s, lambda p, s=s: contrib.at[s, rows_of(p, share_rows)], got_contrib.at[s, me]))
     slot_count = sec_dev * channels
     owner_of = [target_ref[i // channels, i % channels] // sec_dev for i in range(slot_count)]
     for i in range(slot_count):
@@ -115,26 +135,6 @@
 
     lax.fori_loop(0, owners, fill_labels, 0)
     labels = route(lambda p: label_rows.at[p], got_labels.at[here], label_sem, load_sem.at[2])
-    for load in loads:
-        load.wait()
-    for s in range(sec_dev):
-        l_ref[s] = jnp.dot(l_ref[s], psi_ref[s], precision=PRECISE, preferred_element_type=jnp.float32)
-
-    second = []
-    for s in range(sec_dev):
-        arrived(first[s])
-        parts = [gathered(got_right, s, k) for k in range(n)]
-        for a in range(n):
-            total = coup_ref[a, me] * parts[0]
-            for k in range(1, n):
-                total = total + coup_ref[a, lax.rem(me + k, n)] * parts[k]
-            comp_rows[s, a] = total
-        second.append(send(1, s, lambda p, s=s: comp_rows.at[s, p], comp.at[s, rows_of(me, share_rows)]))
-    third = []
-    for s in range(sec_dev):
-        arrived(second[s])
-        contrib[s] = jnp.dot(l_ref[s], comp[s], precision=PRECISE, preferred_element_type=jnp.float32)
-        third.append(send(2, s, lambda p, s=s: contrib.at[s, rows_of(p, share_rows)], got_contrib.at[s, me]))
     for s in range(sec_dev):
         arrived(third[s])
         parts = [gathered(got_contrib, s, k) for k in range(n)]

time: 84.2 us -> 84.2 us (level); the launches traced: 84 us -> 82.7 us
  Pallas kernels: 82.7 us -> 81.4 us
    pallas_call x1, Pallas kernels: 82.7 us -> 81.4 us  [term_stage(): pl.pallas_call(functools.partial(term_kernel, n, owners), out_shape=jax.S...]
where the time goes in v14:
time: 84.2 us; the launch traced here: 82.7 us
  Pallas kernels  81.4 us (97%)
  local copies, waits for them, and re-layouts  1.32 us (2%)
    pallas_call x1, Pallas kernels, term_stage(): pl.pallas_call(functools.partial(term_kernel, n, owners), out_shape=jax.S...  81.4 us

profile of v14, /device:TPU:1, one launch (start us, length us, event | category | flops | bytes accessed | tf_op | source)
XLA Modules:
  0.0 82.7 jit_solution(18037595194121963253)
XLA Ops:
  0.0 81.4 %shard_map.73 = f32[4,8,128]{2,1,0:T(8,128)} custom-call(f32[4,128,128]{2,1,0:T(8,128)} %bitcast.3, f32[4,128,128]{2,1,0:T(8,128)} %bitcast.4, f32[4,128,128]{2,1,0:T(8,128)} %psi_hbm.1, f32[16,16]{1,0:T(8,128)} %coup_ref.1, s32[4,16]{1,0:T(4,128)} %bitcast.5, s32[16]{0:T(128)} %channel_ref.1, s32[4,8]{1,0:T(4,128)} %target_ref.1), custom_call_target="tpu_custom_call" | custom-call | tf_op jit(solution)/shard_map/pallas_call | solution.py:184
  81.4 1.3 %copy.9 = f32[4,8,128]{2,1,0:T(8,128)} copy(f32[4,8,128]{2,1,0:T(8,128)} %shard_map.73) | data formatting | bytes 32768

commit v15 on v11

--- a/solution.py
+++ b/solution.py
@@ -153,7 +153,7 @@
     fourth = route(lambda p: outgoing.at[p], got_slots.at[here], route_sem, load_sem.at[3])
     for copies in (labels, fourth):
         arrived(copies)
-    totals = [None] * sec_dev
+    totals = [[None] * sec_dev for _ in range(capacity)]
     for o in range(owners):
         label_row = got_labels[o]
         for slot in range(capacity):
@@ -161,9 +161,10 @@
             rows = got_slots[o, pl.ds(slot * share_rows, share_rows)]
             for p in range(sec_dev):
                 part = jnp.where(label == float(p + 1), rows, 0.0)
-                totals[p] = part if totals[p] is None else totals[p] + part
-    for p in range(sec_dev):
-        out_ref[p] = totals[p]
+                totals[slot][p] = part if totals[slot][p] is None else totals[slot][p] + part
+    for slot in range(capacity):
+        for p in range(sec_dev):
+            out_ref[slot, p] = totals[slot][p]
     for copies in first + second + third + [labels, fourth]:
         for copy in copies[1:]:
             copy.wait_send()
@@ -183,7 +184,7 @@
     vmem = pl.BlockSpec(memory_space=pltpu.VMEM)
     return pl.pallas_call(
         functools.partial(term_kernel, n, owners),
-        out_shape=jax.ShapeDtypeStruct((sec_dev, share_rows, block_size), jnp.float32),
+        out_shape=jax.ShapeDtypeStruct((capacity, sec_dev, share_rows, block_size), jnp.float32),
         in_specs=[hbm, hbm, hbm, smem, smem, smem, smem],
         out_specs=vmem,
         scratch_shapes=[
@@ -216,7 +217,8 @@
 
 def local(psi_blocks, left_ops, right_ops, couplings, pattern, channel, target):
     owners = lax.axis_size("sector")
-    return term_stage(right_ops[0], left_ops[0], psi_blocks, couplings, pattern.T, channel, target, owners)
+    by_rank = term_stage(right_ops[0], left_ops[0], psi_blocks, couplings, pattern.T, channel, target, owners)
+    return jnp.sum(by_rank, axis=0)
 
 
 def solution(mesh):

time: 84.2 us -> 84.3 us (level)
  other arithmetic: 0 us -> 1.37 us
  local copies, waits for them, and re-layouts: 1.32 us -> 0 us
    reduce_sum x0 -> x1, other arithmetic: none -> 1.37 us  [local(): return jnp.sum(by_rank, axis=0)]
    unnamed x1 -> x0, local copies, waits for them, and re-layouts: 1.32 us -> none
where the time goes in v15:
time: 84.3 us; the launch traced here: 84.1 us
  Pallas kernels  82.7 us (98%)
  other arithmetic  1.37 us (2%)
    pallas_call x1, Pallas kernels, term_stage(): pl.pallas_call(functools.partial(term_kernel, n, owners), out_shape=jax.S...  82.7 us

profile of v15, /device:TPU:1, one launch (start us, length us, event | category | flops | bytes accessed | tf_op | source)
XLA Modules:
  0.0 84.1 jit_solution(8591530471625431507)
XLA Ops:
  0.0 82.7 %shard_map.73 = f32[2,4,8,128]{3,2,1,0:T(8,128)} custom-call(f32[4,128,128]{2,1,0:T(8,128)} %bitcast.3, f32[4,128,128]{2,1,0:T(8,128)} %bitcast.4, f32[4,128,128]{2,1,0:T(8,128)} %psi_hbm.1, f32[16,16]{1,0:T(8,128)} %coup_ref.1, s32[4,16]{1,0:T(4,128)} %bitcast.5, s32[16]{0:T(128)} %channel_ref.1, s32[4,8]{1,0:T(4,128)} %target_ref.1), custom_call_target="tpu_custom_call" | custom-call | tf_op jit(solution)/shard_map/pallas_call | solution.py:185
  82.7 1.4 %reduce_sum.9 = f32[4,8,128]{2,1,0:T(8,128)} reduce(f32[2,4,8,128]{3,2,1,0:T(8,128)} %shard_map.73, f32[]{:T(128)} %constant.0.clone.1), dimensions={0}, to_apply=%region_0.0 | reduce | flops 4096 | bytes 49156 | tf_op jit(solution)/shard_map/reduce_sum | solution.py:221

commit v16 on v11

--- a/solution.py
+++ b/solution.py
@@ -146,11 +146,24 @@
                 total = live * parts[k] if total is None else total + live * parts[k]
             partial[s * channels + c] = total
     partial[sec_dev * channels] = jnp.zeros((share_rows, block_size), jnp.float32)
-    for o in range(owners):
+    fourth = []
+    for k in range(owners):
+        o = lax.rem(here + k, owners)
         for slot in range(capacity):
-            at = o * capacity + slot
-            outgoing[o, pl.ds(slot * share_rows, share_rows)] = partial[source_tab[at]]
-    fourth = route(lambda p: outgoing.at[p], got_slots.at[here], route_sem, load_sem.at[3])
+            outgoing[o, pl.ds(slot * share_rows, share_rows)] = partial[source_tab[o * capacity + slot]]
+        if k == 0:
+            copy = pltpu.make_async_copy(outgoing.at[o], got_slots.at[here], load_sem.at[3])
+        else:
+            copy = pltpu.make_async_remote_copy(
+                src_ref=outgoing.at[o],
+                dst_ref=got_slots.at[here],
+                send_sem=route_sem.at[0, k],
+                recv_sem=route_sem.at[1, k],
+                device_id={"sector": o},
+                device_id_type=MESH,
+            )
+        copy.start()
+        fourth.append(copy)
     for copies in (labels, fourth):
         arrived(copies)
     totals = [None] * sec_dev

time: 84.2 us -> 84.2 us (level)
  no operation moved by 1% of the time
where the time goes in v16:
time: 84.2 us; the launch traced here: 84 us
  Pallas kernels  82.6 us (98%)
  local copies, waits for them, and re-layouts  1.32 us (2%)
    pallas_call x1, Pallas kernels, term_stage(): pl.pallas_call(functools.partial(term_kernel, n, owners), out_shape=jax.S...  82.6 us

profile of v16, /device:TPU:1, one launch (start us, length us, event | category | flops | bytes accessed | tf_op | source)
XLA Modules:
  0.0 84.0 jit_solution(8967796861797230431)
XLA Ops:
  0.0 82.6 %shard_map.73 = f32[4,8,128]{2,1,0:T(8,128)} custom-call(f32[4,128,128]{2,1,0:T(8,128)} %bitcast.3, f32[4,128,128]{2,1,0:T(8,128)} %bitcast.4, f32[4,128,128]{2,1,0:T(8,128)} %psi_hbm.1, f32[16,16]{1,0:T(8,128)} %coup_ref.1, s32[4,16]{1,0:T(4,128)} %bitcast.5, s32[16]{0:T(128)} %channel_ref.1, s32[4,8]{1,0:T(4,128)} %target_ref.1), custom_call_target="tpu_custom_call" | custom-call | tf_op jit(solution)/shard_map/pallas_call | solution.py:197
  82.7 1.3 %copy.9 = f32[4,8,128]{2,1,0:T(8,128)} copy(f32[4,8,128]{2,1,0:T(8,128)} %shard_map.73) | data formatting | bytes 32768

commit v17 on v11

--- a/solution.py
+++ b/solution.py
@@ -9,7 +9,7 @@
 
 MESH = pl.DeviceIdType.MESH
 
-PRECISE = lax.Precision.HIGHEST
+PRECISE = lax.Precision.HIGH
 
 
 def rows_of(index, share_rows):

time: 84.2 us -> 84.2 us (level)
  no operation moved by 1% of the time
where the time goes in v17:
time: 84.2 us; the launch traced here: 83.9 us
  Pallas kernels  82.6 us (98%)
  local copies, waits for them, and re-layouts  1.32 us (2%)
    pallas_call x1, Pallas kernels, term_stage(): pl.pallas_call(functools.partial(term_kernel, n, owners), out_shape=jax.S...  82.6 us

profile of v17, /device:TPU:1, one launch (start us, length us, event | category | flops | bytes accessed | tf_op | source)
XLA Modules:
  0.0 83.9 jit_solution(15695694706783927592)
XLA Ops:
  0.0 82.6 %shard_map.73 = f32[4,8,128]{2,1,0:T(8,128)} custom-call(f32[4,128,128]{2,1,0:T(8,128)} %bitcast.3, f32[4,128,128]{2,1,0:T(8,128)} %bitcast.4, f32[4,128,128]{2,1,0:T(8,128)} %psi_hbm.1, f32[16,16]{1,0:T(8,128)} %coup_ref.1, s32[4,16]{1,0:T(4,128)} %bitcast.5, s32[16]{0:T(128)} %channel_ref.1, s32[4,8]{1,0:T(4,128)} %target_ref.1), custom_call_target="tpu_custom_call" | custom-call | tf_op jit(solution)/shard_map/pallas_call | solution.py:184
  82.6 1.3 %copy.9 = f32[4,8,128]{2,1,0:T(8,128)} copy(f32[4,8,128]{2,1,0:T(8,128)} %shard_map.73) | data formatting | bytes 32768

commit v18 on v11

--- a/solution.py
+++ b/solution.py
@@ -114,7 +114,6 @@
         return carry
 
     lax.fori_loop(0, owners, fill_labels, 0)
-    labels = route(lambda p: label_rows.at[p], got_labels.at[here], label_sem, load_sem.at[2])
     for load in loads:
         load.wait()
     for s in range(sec_dev):
@@ -135,6 +134,7 @@
         arrived(second[s])
         contrib[s] = jnp.dot(l_ref[s], comp[s], precision=PRECISE, preferred_element_type=jnp.float32)
         third.append(send(2, s, lambda p, s=s: contrib.at[s, rows_of(p, share_rows)], got_contrib.at[s, me]))
+    labels = route(lambda p: label_rows.at[p], got_labels.at[here], label_sem, load_sem.at[2])
     for s in range(sec_dev):
         arrived(third[s])
         parts = [gathered(got_contrib, s, k) for k in range(n)]

time: 84.2 us -> 84.5 us (level)
  the two profiles are of different devices: /device:TPU:1 before, /device:TPU:6 now
where the time goes in v18:
time: 84.5 us; the launch traced here: 84.3 us
  Pallas kernels  82.9 us (98%)
  local copies, waits for them, and re-layouts  1.32 us (2%)
    pallas_call x1, Pallas kernels, term_stage(): pl.pallas_call(functools.partial(term_kernel, n, owners), out_shape=jax.S...  82.9 us

profile of v18, /device:TPU:6, one launch (start us, length us, event | category | flops | bytes accessed | tf_op | source)
XLA Modules:
  0.0 84.3 jit_solution(8934795325191201167)
XLA Ops:
  0.0 82.9 %shard_map.73 = f32[4,8,128]{2,1,0:T(8,128)} custom-call(f32[4,128,128]{2,1,0:T(8,128)} %bitcast.3, f32[4,128,128]{2,1,0:T(8,128)} %bitcast.4, f32[4,128,128]{2,1,0:T(8,128)} %psi_hbm.1, f32[16,16]{1,0:T(8,128)} %coup_ref.1, s32[4,16]{1,0:T(4,128)} %bitcast.5, s32[16]{0:T(128)} %channel_ref.1, s32[4,8]{1,0:T(4,128)} %target_ref.1), custom_call_target="tpu_custom_call" | custom-call | tf_op jit(solution)/shard_map/pallas_call | solution.py:184
  83.0 1.3 %copy.9 = f32[4,8,128]{2,1,0:T(8,128)} copy(f32[4,8,128]{2,1,0:T(8,128)} %shard_map.73) | data formatting | bytes 32768
